TPU v7x, 32 devices: a whole 2x2x4 slice. The times are simulated.
32 devices in a mesh: tm: 4 (over z), space: 8 (over y, x, core).
Axes of the slice: x: 2, y: 2, z: 4, core: 2. Of those that a mesh axis runs over, the one named last changes fastest.
Arguments:
- iterate: float32 [4, 8, 16, 16, 512], P('tm', 'space'), may hold values from -3 to 3
- source_term: float32 [4, 8, 16, 16, 512], P('tm', 'space'), may hold values from -6 to 6
- conductivity: float32 [8, 16, 16, 512], P('space'), may hold values from 0.5 to 4
Outputs:
- new_iterate: float32 [4, 8, 16, 16, 512], P('tm', 'space')
- residual: float32 [4, 8, 16, 16, 512], P('tm', 'space')
All inputs are finite; a program needn't handle non-finite values.
Results may differ from a plain program's by a relative error of at most 0.00002.
Values sent between devices are 32-bit elements; how exact they have to be, the bound alone decides.
A program may use at most 64 MiB of HBM per device.

v0:
```python
import functools

import jax
import jax.numpy as jnp
from jax import lax
from jax.experimental import pallas as pl
from jax.experimental.pallas import tpu as pltpu
from jax.sharding import PartitionSpec as P

tau_step = 0.08
damping = 0.7
group = 4
pad = 8
mesh_ids = pl.DeviceIdType.MESH

slots_state = [0, 2, 4, 6]
slots_one = [8, 9, 10, 11]
slots_two = [12, 13, 14, 15]
slots_mid_one = [16, 17]
slots_mid_two = [18, 19]
slot_top = 20
n_slots = 21
parts = 2
pace = {"one": 2, "two": 1, "mid_one": 1, "mid_two": 1, "top": 1}


def kernel(
    tm_size, space_size,
    state_in, source_in, kappa_in, new_out, res_out,
    u, c, e1, e2, kap, src, res, wl, wr, rd,
    mc, me1, me2, mb, mwl, mwr, mrd, tc, te, tb, new,
    row_send, row_recv, col_send, col_recv, own, beside, edge_send, edge_recv,
    in_ssem, in_rsem, out_ssem, out_rsem, out_lsem, in_lsem, e_ssem, e_rsem, loc_sem, h_ssem, h_rsem, t_ssem, t_rsem,
):
    nz, tx, width = kap.shape
    real = pl.ds(pad, tx)
    low = pl.ds(pad - 1, tx)
    high = pl.ds(pad + 1, tx)
    planes = pl.ds(1, nz)
    me = lax.axis_index("tm")
    sp = lax.axis_index("space")
    q = me % group
    base = me - q
    chained = tm_size > group
    has_dn, has_up = sp > 0, sp < space_size - 1
    has_left, has_right = q > 0, q < group - 1
    has_prev, has_next = base > 0, base + group < tm_size
    sides = [
        (has_dn, {"space": sp - 1}),
        (has_up, {"space": sp + 1}),
        (has_left, {"tm": me - 1}),
        (has_right, {"tm": me + 1}),
    ]

    def zero_edges(ref, count):
        for n in range(count):
            for plane in (0, nz + 1):
                ref[n, plane] = jnp.zeros(ref.shape[2:], jnp.float32)

    def columns(d):
        return pl.ds(pl.multiple_of(d * width, width), width)

    kappa_copy = pltpu.make_async_copy(kappa_in.at[0, :, :, columns(q)], kap, loc_sem.at[2])
    own_copy = pltpu.make_async_copy(state_in.at[0, 0], own, loc_sem.at[5])

    def beside_copy(side):
        block = kappa_in.at[0, :, :, columns(q - 1 + 2 * side)]
        return pltpu.make_async_copy(block, beside.at[side], loc_sem.at[6 + side])

    own_copy.start()
    kappa_copy.start()
    for side in range(2):

        @pl.when(sides[2 + side][0])
        def _():
            beside_copy(side).start()

    barrier = pltpu.get_barrier_semaphore()
    for j in range(1, group):
        pl.semaphore_signal(
            barrier, inc=1, device_id={"tm": base + (q + j) % group}, device_id_type=mesh_ids
        )
    greeted = [(has_dn, sides[0][1]), (has_up, sides[1][1])]
    if chained:
        greeted += [(has_prev, {"tm": me - group}), (has_next, {"tm": me + group})]
    for has, where in greeted:

        @pl.when(has)
        def _():
            pl.semaphore_signal(barrier, inc=1, device_id=where, device_id_type=mesh_ids)

    expected = group - 1
    for has, _ in greeted:
        expected = expected + jnp.where(has, 1, 0)
    pl.semaphore_wait(barrier, expected)

    def in_copy(a, j):
        d = (q + j) % group
        if a == 0:
            hbm, dst = state_in.at[0, 0, :, :, columns(d)], u.at[q + 1, planes, real, :]
        else:
            some = pl.ds((a - 1) * (nz // parts), nz // parts)
            hbm, dst = source_in.at[0, 0, some, :, columns(d)], src.at[q, some]
        if j == 0:
            return pltpu.make_async_copy(hbm, dst, in_lsem.at[a])
        return pltpu.make_async_remote_copy(
            src_ref=hbm, dst_ref=dst, send_sem=in_ssem.at[a, j - 1],
            recv_sem=in_rsem.at[a, j - 1], device_id={"tm": base + d}, device_id_type=mesh_ids,
        )

    def out_copy(a, j, part):
        d = (q + j) % group
        some = pl.ds(part * (nz // parts), nz // parts)
        hbm = (res_out, new_out)[a].at[0, 0, some, :, columns(q)]
        held = (res, new)[a].at[d, some]
        if j == 0:
            return pltpu.make_async_copy(held, hbm, out_lsem.at[a, part])
        return pltpu.make_async_remote_copy(
            src_ref=held, dst_ref=hbm, send_sem=out_ssem.at[a, part, j - 1],
            recv_sem=out_rsem.at[a, part, j - 1], device_id={"tm": base + d},
            device_id_type=mesh_ids,
        )

    order = (2, 1, 3, 0)
    for j in order:
        in_copy(0, j).start()

    zero_edges(u, group + 1)
    zero_edges(c, group)
    zero_edges(e1, group + 1)
    zero_edges(e2, group + 1)
    zero_edges(mc, 2)
    zero_edges(me1, 3)
    zero_edges(me2, 3)
    zero_edges(tc, 1)
    zero_edges(te, 2)

    @pl.when(jnp.logical_not(has_prev))
    def _():
        for ref in (u, e1, e2, me1, me2, te):
            ref[0] = jnp.zeros(ref.shape[1:], jnp.float32)

    for number, (has, _) in enumerate(sides):
        buffer = row_recv if number < 2 else col_recv

        @pl.when(jnp.logical_not(has))
        def _():
            buffer[number % 2] = jnp.zeros(buffer.shape[1:], jnp.float32)

    for side in range(2):

        @pl.when(jnp.logical_not(sides[2 + side][0]))
        def _():
            beside[side] = jnp.zeros(beside.shape[1:], jnp.float32)

    lane = lax.broadcasted_iota(jnp.int32, (tx, width), 1)
    blank = jnp.zeros((tx, width), jnp.float32)

    def pack_sides(p, left, right, packed):
        if left is not None:
            packed = jnp.where(lane == 2 * p + 1, pltpu.roll(left, 2 * p + 2, 1), packed)
        if right is not None:
            packed = jnp.where(lane == 2 * p, pltpu.roll(right, 2 * p, 1), packed)
        return packed

    def pack_body(p, packed):
        blocks = [own[p, :, d * width : (d + 1) * width] for d in range(group)]
        return tuple(
            pack_sides(
                p, blocks[d - 1] if d else None,
                blocks[d + 1] if d < group - 1 else None, packed[d],
            )
            for d in range(group)
        )

    own_copy.wait()
    packed = lax.fori_loop(0, nz, pack_body, (blank,) * group, unroll=4)
    for d in range(group):
        edge_send[d] = packed[d]
    edge_recv[q] = edge_send[q]

    def edge_copy(j):
        d = (q + j) % group
        return pltpu.make_async_remote_copy(
            src_ref=edge_send.at[d], dst_ref=edge_recv.at[q], send_sem=e_ssem.at[j - 1],
            recv_sem=e_rsem.at[j - 1], device_id={"tm": base + d}, device_id_type=mesh_ids,
        )

    for j in order[:3]:
        edge_copy(j).start()
    for part in range(parts):
        for j in order:
            in_copy(1 + part, j).start()

    def halo_copy(slot, count, number):
        part = pl.ds(slot, count)
        opposite = number ^ 1
        if number < 2:
            source, target = row_send.at[number, part], row_recv.at[opposite, part]
        else:
            source, target = col_send.at[part], col_recv.at[opposite - 2, part]
        return pltpu.make_async_remote_copy(
            src_ref=source, dst_ref=target, send_sem=h_ssem.at[number, slot],
            recv_sem=h_rsem.at[opposite, slot], device_id=sides[number][1],
            device_id_type=mesh_ids,
        )

    def halo_send(slot, count=1, which=(2, 3, 0, 1)):
        for number in which:

            @pl.when(sides[number][0])
            def _():
                halo_copy(slot, count, number).start()

    def halo_wait(slot, count=1, which=(2, 3, 0, 1)):
        part = pl.ds(slot, count)
        for number in which:
            target = row_recv.at[number, part] if number < 2 else col_recv.at[number - 2, part]

            @pl.when(sides[number][0])
            def _():
                pltpu.make_async_remote_copy(
                    src_ref=target, dst_ref=target, send_sem=h_ssem.at[number, slot],
                    recv_sem=h_rsem.at[number, slot], device_id=sides[number][1],
                    device_id_type=mesh_ids,
                ).wait_recv()

    def time_copy(number, ref, last):
        return pltpu.make_async_remote_copy(
            src_ref=ref.at[last, planes, real, :], dst_ref=ref.at[0, planes, real, :],
            send_sem=t_ssem.at[number],
            recv_sem=t_rsem.at[number], device_id={"tm": me + group}, device_id_type=mesh_ids,
        )

    time_refs = [(u, group), (e1, group), (e2, group), (me1, 2), (me2, 2), (te, 1)]

    def time_send(number):
        if chained:

            @pl.when(has_next)
            def _():
                time_copy(number, *time_refs[number]).start()

    def time_wait(number):
        if chained:

            @pl.when(has_prev)
            def _():
                time_copy(number, *time_refs[number]).wait_recv()

    first_lane = lane == 0
    last_lane = lane == width - 1
    odd_lane = lane % 2 == 1
    pair_lane = lane // 2

    def put_send(slot, p, value):
        row_send[0, slot, pl.ds(p, 1), :] = value[:1]
        row_send[1, slot, pl.ds(p, 1), :] = value[tx - 1 :]

    def pack(slot, p, value, packed):
        put_send(slot, p, value)
        return jnp.where(pair_lane == p, pltpu.roll(value, 2 * p + 1, 1), packed)

    def ghosts(slot):
        return jnp.where(
            odd_lane,
            pltpu.roll(col_recv[0, slot], 1, 1),
            pltpu.roll(col_recv[1, slot], width - 1, 1),
        )

    def put_rows(ref, n, slot, p):
        ref[n, p + 1, pl.ds(pad - 1, 1), :] = row_recv[0, slot, pl.ds(p, 1), :]
        ref[n, p + 1, pl.ds(pad + tx, 1), :] = row_recv[1, slot, pl.ds(p, 1), :]

    def sideways(value, ghost, p):
        edge = pltpu.roll(ghost, width - 1 - 2 * p, 1)
        left = jnp.where(first_lane, edge, pltpu.roll(value, 1, 1))
        right = jnp.where(last_lane, edge, pltpu.roll(value, width - 1, 1))
        return left, right

    def straight(ref, n, p):
        return (
            ref[n, p + 1, low, :], ref[n, p + 1, high, :],
            ref[n, p, real, :], ref[n, p + 2, real, :],
        )

    def flux(v, v_near, cc, c_near, left_w, right_w):
        total = left_w * (v - v_near[4]) + right_w * (v - v_near[5])
        for i in range(4):
            total = total + (cc + c_near[i]) * (v - v_near[i])
        return total

    def near_of(ref, n, slot, ghost, p):
        put_rows(ref, n, slot, p)
        v = ref[n, p + 1, real, :]
        return v, straight(ref, n, p) + sideways(v, ghost, p)

    def plane_loop(body, init):
        return lax.fori_loop(0, nz, body, init, unroll=8)

    for side in range(2):

        @pl.when(sides[2 + side][0])
        def _():
            beside_copy(side).wait()

    def kappa_body(p, packed):
        return pack_sides(p, beside[0, p], beside[1, p], packed)

    kappa_edge = lax.fori_loop(0, nz, kappa_body, blank, unroll=4)

    kappa_copy.wait()
    in_copy(0, 0).wait()
    for j in order[:3]:
        in_copy(0, j).wait_recv()
    time_send(0)
    for n in range(group):

        def body(p, carry):
            v = u[n + 1, p + 1, real, :]
            cc = kap[p] * (1.0 + v * v)
            c[n, p + 1, real, :] = cc
            put_send(slots_state[n], p, v)
            put_send(slots_state[n] + 1, p, cc)
            return carry

        plane_loop(body, 0)
        halo_send(slots_state[n], 2, (0, 1))

    time_wait(0)
    for j in order[:3]:
        edge_copy(j).wait_recv()
    half = 0.5 * tau_step
    for n in range(group):
        halo_wait(slots_state[n], 2, (0, 1))
        ghost_c = kappa_edge * (1.0 + edge_recv[n] * edge_recv[n])

        ghost_u = edge_recv[n]

        def body(p, carry):
            cc, c_near = near_of(c, n, slots_state[n] + 1, ghost_c, p)
            left_w, right_w = cc + c_near[4], cc + c_near[5]
            wl[n, p], wr[n, p] = left_w, right_w
            total = 6.0 * cc
            for item in c_near:
                total = total + item
            rd[n, p] = damping / (1.0 + half * total)
            v, v_near = near_of(u, n + 1, slots_state[n], ghost_u, p)
            total = flux(v, v_near, cc, c_near, left_w, right_w)
            res[n, p] = v - u[n, p + 1, real, :] + half * total
            return carry

        plane_loop(body, 0)

    for part in range(parts):
        in_copy(1 + part, 0).wait()
        for j in order[:3]:
            in_copy(1 + part, j).wait_recv()
        for n in range(group):

            def body(p, packed):
                left = src[n, p] - res[n, p]
                res[n, p] = left
                update = left * rd[n, p]
                e1[n + 1, p + 1, real, :] = update
                return pack(slots_one[n], p, update, packed)

            first = part * (nz // parts)
            packed = col_send[slots_one[n]] if part else blank
            col_send[slots_one[n]] = lax.fori_loop(
                first, first + nz // parts, body, packed, unroll=True
            )
            if part == parts - 1:
                halo_send(slots_one[n])
    time_send(1)

    pieces = [(j, part) for part in range(parts) for j in order]
    remote_pieces = [piece for piece in pieces if piece[0]]
    for part in range(parts):
        out_copy(0, 0, part).start()

    def give(stage):
        for _ in range(pace[stage]):
            out_copy(0, *remote_pieces.pop(0)).start()

    give("one")

    time_wait(1)
    for n in range(group):
        halo_wait(slots_one[n])
        ghost = ghosts(slots_one[n])

        def body(p, packed):
            v, v_near = near_of(e1, n + 1, slots_one[n], ghost, p)
            total = flux(v, v_near, c[n, p + 1, real, :], straight(c, n, p), wl[n, p], wr[n, p])
            left = res[n, p] - (v - e1[n, p + 1, real, :] + half * total)
            update = v + left * rd[n, p]
            e2[n + 1, p + 1, real, :] = update
            return pack(slots_two[n], p, update, packed)

        col_send[slots_two[n]] = plane_loop(body, blank)
        halo_send(slots_two[n])
    time_send(2)
    give("two")

    def body(p, carry):
        for j in range(2):
            mc[j, p + 1] = 0.5 * (c[2 * j, p + 1] + c[2 * j + 1, p + 1])
            mwl[j, p] = 0.5 * (wl[2 * j, p] + wl[2 * j + 1, p])
            mwr[j, p] = 0.5 * (wr[2 * j, p] + wr[2 * j + 1, p])
        tc[0, p + 1] = 0.5 * (mc[0, p + 1] + mc[1, p + 1])
        return carry

    lax.fori_loop(0, nz, body, 0)

    def diagonal(ref, j, p, left_w, right_w, scale):
        cc = ref[j, p + 1, real, :]
        total = 4.0 * cc + left_w + right_w
        for item in straight(ref, j, p):
            total = total + item
        return damping / (1.0 + scale * total)

    time_wait(2)
    for j in range(2):
        halo_wait(slots_two[2 * j])
        halo_wait(slots_two[2 * j + 1])
        pair = [ghosts(slots_two[2 * j]), ghosts(slots_two[2 * j + 1])]

        def body(p, packed):
            rhs = None
            for i in range(2):
                n = 2 * j + i
                v, v_near = near_of(e2, n + 1, slots_two[n], pair[i], p)
                total = flux(
                    v, v_near, c[n, p + 1, real, :], straight(c, n, p), wl[n, p], wr[n, p]
                )
                left = res[n, p] - (v - e2[n, p + 1, real, :] + half * total)
                rhs = left if rhs is None else rhs + left
            inverse = diagonal(mc, j, p, mwl[j, p], mwr[j, p], 2.0 * half)
            mrd[j, p] = inverse
            mb[j, p] = rhs
            update = rhs * inverse
            me1[j + 1, p + 1, real, :] = update
            return pack(slots_mid_one[j], p, update, packed)

        col_send[slots_mid_one[j]] = plane_loop(body, blank)
        halo_send(slots_mid_one[j])
    time_send(3)
    give("mid_one")

    time_wait(3)
    for j in range(2):
        halo_wait(slots_mid_one[j])
        ghost = ghosts(slots_mid_one[j])

        def body(p, packed):
            v, v_near = near_of(me1, j + 1, slots_mid_one[j], ghost, p)
            total = flux(v, v_near, mc[j, p + 1, real, :], straight(mc, j, p), mwl[j, p], mwr[j, p])
            left = mb[j, p] - (v - me1[j, p + 1, real, :] + 2.0 * half * total)
            update = v + left * mrd[j, p]
            me2[j + 1, p + 1, real, :] = update
            return pack(slots_mid_two[j], p, update, packed)

        col_send[slots_mid_two[j]] = plane_loop(body, blank)
        halo_send(slots_mid_two[j])
    time_send(4)
    give("mid_two")

    time_wait(4)
    for j in range(2):
        halo_wait(slots_mid_two[j])
    pair = [ghosts(slots_mid_two[j]) for j in range(2)]

    def top_weights(p):
        return 0.5 * (mwl[0, p] + mwl[1, p]), 0.5 * (mwr[0, p] + mwr[1, p])

    def body(p, packed):
        rhs = None
        for j in range(2):
            v, v_near = near_of(me2, j + 1, slots_mid_two[j], pair[j], p)
            total = flux(v, v_near, mc[j, p + 1, real, :], straight(mc, j, p), mwl[j, p], mwr[j, p])
            left = mb[j, p] - (v - me2[j, p + 1, real, :] + 2.0 * half * total)
            rhs = left if rhs is None else rhs + left
        tb[p] = rhs
        update = rhs * diagonal(tc, 0, p, *top_weights(p), 4.0 * half)
        te[1, p + 1, real, :] = update
        return pack(slot_top, p, update, packed)

    col_send[slot_top] = plane_loop(body, blank)
    halo_send(slot_top)
    time_send(5)
    give("top")
    time_wait(5)
    halo_wait(slot_top)
    ghost = ghosts(slot_top)

    def body(p, carry):
        v, v_near = near_of(te, 1, slot_top, ghost, p)
        weights = top_weights(p)
        total = flux(v, v_near, tc[0, p + 1, real, :], straight(tc, 0, p), *weights)
        left = tb[p] - (v - te[0, p + 1, real, :] + 4.0 * half * total)
        update = v + left * diagonal(tc, 0, p, *weights, 4.0 * half)
        for n in range(group):
            mid = me2[n // 2 + 1, p + 1, real, :] + update
            new[n, p] = u[n + 1, p + 1, real, :] + (e2[n + 1, p + 1, real, :] + mid)
        return carry

    for part in range(parts):
        first = part * (nz // parts)
        lax.fori_loop(first, first + nz // parts, body, 0, unroll=True)
        for j in order:
            out_copy(1, j, part).start()

    for j in order[:3]:
        edge_copy(j).wait_send()

    for a in range(1 + parts):
        for j in order[:3]:
            in_copy(a, j).wait_send()
    halos = [(slot, 2, (0, 1)) for slot in slots_state]
    halos += [(slot, 1, (0, 1, 2, 3)) for slot in range(slots_one[0], n_slots)]
    for slot, count, which in halos:
        for number in which:

            @pl.when(sides[number][0])
            def _():
                halo_copy(slot, count, number).wait_send()

    if chained:

        @pl.when(has_next)
        def _():
            for number, (ref, last) in enumerate(time_refs):
                time_copy(number, ref, last).wait_send()

    for a in range(2):
        for j, part in pieces:
            if j == 0:
                out_copy(a, j, part).wait()
            else:
                out_copy(a, j, part).wait_send()
                out_copy(a, j, part).wait_recv()


def shards(tm_size, space_size, iterate, source_term, conductivity):
    _, nz, tx, ty = conductivity.shape
    width = ty // group
    rows = tx + 2 * pad
    f32 = jnp.float32

    def padded(count):
        return pltpu.VMEM((count, nz + 2, rows, width), f32)

    def plain(*lead):
        return pltpu.VMEM((*lead, nz, tx, width), f32)

    dma = pltpu.SemaphoreType.DMA
    out = jax.ShapeDtypeStruct(iterate.shape, f32)
    hbm = pl.BlockSpec(memory_space=pltpu.HBM)
    return pl.pallas_call(
        functools.partial(kernel, tm_size, space_size),
        out_shape=(out, out),
        in_specs=[hbm] * 3,
        out_specs=(hbm, hbm),
        scratch_shapes=[
            padded(group + 1), padded(group), padded(group + 1), padded(group + 1),
            plain(), plain(group), plain(group), plain(group), plain(group), plain(group),
            padded(2), padded(3), padded(3), plain(2), plain(2), plain(2), plain(2),
            padded(1), padded(2), plain(), plain(group),
            pltpu.VMEM((2, n_slots, nz, width), f32), pltpu.VMEM((2, n_slots, nz, width), f32),
            pltpu.VMEM((n_slots, tx, width), f32), pltpu.VMEM((2, n_slots, tx, width), f32),
            pltpu.VMEM((nz, tx, ty), f32), plain(2),
            pltpu.VMEM((group, tx, width), f32), pltpu.VMEM((group, tx, width), f32),
            dma((1 + parts, group - 1)), dma((1 + parts, group - 1)),
            dma((2, parts, group - 1)), dma((2, parts, group - 1)), dma((2, parts)), dma((1 + parts,)),
            dma((group - 1,)), dma((group - 1,)), dma((8,)), dma((4, n_slots)), dma((4, n_slots)), dma((6,)), dma((6,)),
        ],
        compiler_params=pltpu.CompilerParams(
            collective_id=0, has_side_effects=True, vmem_limit_bytes=67043328
        ),
    )(iterate, source_term, conductivity)


def solution(mesh):
    tiled = P("tm", "space", None, None, None)
    in_specs = (tiled, tiled, P("space", None, None, None))
    body = functools.partial(shards, mesh.shape["tm"], mesh.shape["space"])
    return jax.shard_map(
        body, mesh=mesh, in_specs=in_specs, out_specs=(tiled, tiled), check_vma=False
    )
```

profile of v0, /device:TPU:5, one launch (start us, length us, event | category | flops | bytes accessed | tf_op | source)
XLA Modules:
  0.0 64.4 jit_solution(17059818354720840332)
XLA Ops:
  0.6 61.0 %shard_map.50 = (f32[1,1,16,16,512]{4,3,2,1,0:T(8,128)}, f32[1,1,16,16,512]{4,3,2,1,0:T(8,128)}) custom-call(f32[1,1,16,16,512]{4,3,2,1,0:T(8,128)} %state_in.1, f32[1,1,16,16,512]{4,3,2,1,0:T(8,128)} %source_in.1, f32[1,16,16,512]{3,2,1,0:T(8,128)} %kappa_in.1), custom_call_target="tpu_custom_call" | custom-call | tf_op jit(solution)/shard_map/pallas_call | solution.py:560
  61.6 0.0 copy-start
  61.6 1.9 %copy.7 = f32[1,1,16,16,512]{4,3,2,1,0:T(8,128)} copy(f32[1,1,16,16,512]{4,3,2,1,0:T(8,128)} %get-tuple-element.4) | data formatting | bytes 1048576
  63.6 0.0 copy-done
  63.6 0.8 %copy.8 = f32[1,1,16,16,512]{4,3,2,1,0:T(8,128)} copy(f32[1,1,16,16,512]{4,3,2,1,0:T(8,128)S(1)} %copy-done) | data formatting | bytes 1048576
Async XLA Ops:
  61.6 2.0 %copy-start = (f32[1,1,16,16,512]{4,3,2,1,0:T(8,128)S(1)}, f32[1,1,16,16,512]{4,3,2,1,0:T(8,128)}, u32[]{:S(2)}) copy-start(f32[1,1,16,16,512]{4,3,2,1,0:T(8,128)} %get-tuple-element.5) | copy-start | bytes 1572868
where the time goes:
time: 65.7 us; the launch traced here: 64.4 us
  Pallas kernels  61 us (93%)
  local copies, waits for them, and re-layouts  2.74 us (4%)
    pallas_call x1, Pallas kernels, shards(): pl.pallas_call(functools.partial(kernel, tm_size, space_size), out_shape=...  61 us
    unnamed x4, local copies, waits for them, and re-layouts  2.74 us

commit v1 on v0

v1 whole, which is shorter than its diff:
```python
import functools
import types

import jax
import jax.numpy as jnp
from jax import lax
from jax.experimental import pallas as pl
from jax.experimental.pallas import tpu as pltpu
from jax.sharding import PartitionSpec as P

tau_step = 0.08
damping = 0.7
group = 4
halo = 8
pad = 2 * halo
parts = 2
mesh_ids = pl.DeviceIdType.MESH
order = (2, 1, 3, 0)
unroll = 4


def kernel(tm_size, space_size, names, *refs):
    r = types.SimpleNamespace(**dict(zip(names, refs)))
    nz, _, width = r.packed.shape[1], None, r.kap.shape[-1]
    tx = r.state_in.shape[3]
    span = width // nz
    chained = tm_size > group
    half = 0.5 * tau_step
    piece = nz // parts

    full = (pad - halo, tx + 2 * halo)
    trim = (pad - halo // 2, tx + halo)
    core = (pad, tx)

    def rows(win, shift=0):
        return pl.ds(win[0] + shift, win[1])

    real = rows(core)
    planes = pl.ds(1, nz)
    me = lax.axis_index("tm")
    sp = lax.axis_index("space")
    q = me % group
    base = me - q
    has_dn, has_up = sp > 0, sp < space_size - 1
    has_left, has_right = q > 0, q < group - 1
    has_prev, has_next = base > 0, base + group < tm_size
    flanks = [(has_dn, {"space": sp - 1}), (has_up, {"space": sp + 1})]
    beside_has = [has_left, has_right]

    def columns(d):
        return pl.ds(pl.multiple_of(d * width, width), width)

    own_copies = [
        pltpu.make_async_copy(hbm.at[0, 0], r.own.at[f], r.loc_sem.at[f])
        for f, hbm in enumerate((r.state_in, r.source_in))
    ]
    kappa_copy = pltpu.make_async_copy(
        r.kappa_in.at[0, :, :, columns(q)], r.kap.at[:, real, :], r.loc_sem.at[2]
    )

    def beside_copy(side):
        block = r.kappa_in.at[0, :, :, columns(q - 1 + 2 * side)]
        return pltpu.make_async_copy(block, r.beside.at[side], r.loc_sem.at[3 + side])

    own_copies[0].start()
    kappa_copy.start()
    for side in range(2):

        @pl.when(beside_has[side])
        def _():
            beside_copy(side).start()

    own_copies[1].start()

    barrier = pltpu.get_barrier_semaphore()
    for j in range(1, group):
        pl.semaphore_signal(
            barrier, inc=1, device_id={"tm": base + (q + j) % group}, device_id_type=mesh_ids
        )
    greeted = list(flanks)
    if chained:
        greeted += [(has_prev, {"tm": me - group}), (has_next, {"tm": me + group})]
    for has, where in greeted:

        @pl.when(has)
        def _():
            pl.semaphore_signal(barrier, inc=1, device_id=where, device_id_type=mesh_ids)

    expected = group - 1
    for has, _ in greeted:
        expected = expected + jnp.where(has, 1, 0)
    pl.semaphore_wait(barrier, expected)

    def in_copy(a, j):
        d = (q + j) % group
        if a == 0:
            hbm, dst = r.state_in.at[0, 0, :, :, columns(d)], r.u.at[q + 1, planes, real, :]
        else:
            some = pl.ds((a - 1) * piece, piece)
            hbm, dst = r.source_in.at[0, 0, some, :, columns(d)], r.src.at[q, some, real, :]
        if j == 0:
            return pltpu.make_async_copy(hbm, dst, r.in_lsem.at[a])
        return pltpu.make_async_remote_copy(
            src_ref=hbm, dst_ref=dst, send_sem=r.in_ssem.at[a, j - 1],
            recv_sem=r.in_rsem.at[a, j - 1], device_id={"tm": base + d}, device_id_type=mesh_ids,
        )

    def out_copy(a, j, part):
        d = (q + j) % group
        some = pl.ds(part * piece, piece)
        hbm = (r.res_out, r.new_out)[a].at[0, 0, some, :, columns(q)]
        held = (r.res, r.new)[a].at[d, some, real, :]
        if j == 0:
            return pltpu.make_async_copy(held, hbm, r.out_lsem.at[a, part])
        return pltpu.make_async_remote_copy(
            src_ref=held, dst_ref=hbm, send_sem=r.out_ssem.at[a, part, j - 1],
            recv_sem=r.out_rsem.at[a, part, j - 1], device_id={"tm": base + d},
            device_id_type=mesh_ids,
        )

    def strip_copy(f, j):
        d = (q + j) % group
        return pltpu.make_async_remote_copy(
            src_ref=r.strip_send.at[f, d], dst_ref=r.strip_in.at[f, q, :, real, :],
            send_sem=r.strip_ssem.at[f, j - 1], recv_sem=r.strip_rsem.at[f, j - 1],
            device_id={"tm": base + d}, device_id_type=mesh_ids,
        )

    def edge_ref(kind, n, where):
        if kind == 0:
            return r.u.at[n + 1, planes, where, :]
        if kind <= parts:
            return r.src.at[n, pl.ds((kind - 1) * piece, piece), where, :]
        if kind <= parts + 2:
            return r.strip_in.at[kind - parts - 1, n, :, where, :]
        if kind == parts + 3:
            return r.kap.at[:, where, :]
        return r.kap_strip.at[:, where, :]

    def edge_copy(kind, n, number):
        if number == 0:
            source, target = pl.ds(pad, halo), pl.ds(pad + tx, halo)
        else:
            source, target = pl.ds(pad + tx - halo, halo), pl.ds(pad - halo, halo)
        return pltpu.make_async_remote_copy(
            src_ref=edge_ref(kind, n, source), dst_ref=edge_ref(kind, n, target),
            send_sem=r.edge_ssem.at[kind, n, number], recv_sem=r.edge_rsem.at[kind, n, number],
            device_id=flanks[number][1], device_id_type=mesh_ids,
        )

    def edge_start(kind, n=0):
        for number in range(2):

            @pl.when(flanks[number][0])
            def _():
                edge_copy(kind, n, number).start()

    def edge_wait(kind, n=0, send=False):
        for number in range(2):

            @pl.when(flanks[number][0])
            def _():
                if send:
                    edge_copy(kind, n, number).wait_send()
                else:
                    edge_copy(kind, n, 1 - number).wait_recv()

    def edge_recv_wait(kind, n=0):
        for number in range(2):

            @pl.when(flanks[number][0])
            def _():
                edge_copy(kind, n, 1 - number).wait_recv()

    time_refs = [(r.u, group), (r.e1, group), (r.e2, group), (r.me1, 2), (r.me2, 2), (r.te, 1)]
    time_strips = [
        (r.su, group), (r.se1, group), (r.se2, group), (r.sme1, 2), (r.sme2, 2), (r.ste, 1),
    ]

    def time_copies(number):
        made = []
        for kind, (ref, last) in enumerate((time_refs[number], time_strips[number])):
            middle = planes if kind == 0 else pl.ds(0, 2)
            made.append(
                pltpu.make_async_remote_copy(
                    src_ref=ref.at[last, middle, rows(full), :],
                    dst_ref=ref.at[0, middle, rows(full), :],
                    send_sem=r.time_ssem.at[number, kind], recv_sem=r.time_rsem.at[number, kind],
                    device_id={"tm": me + group}, device_id_type=mesh_ids,
                )
            )
        return made

    def time_send(number):
        if chained:

            @pl.when(has_next)
            def _():
                for copy in time_copies(number):
                    copy.start()

    def time_wait(number):
        if chained:

            @pl.when(has_prev)
            def _():
                for copy in time_copies(number):
                    copy.wait_recv()

    for j in order:
        in_copy(0, j).start()
    kappa_copy.wait()
    kappa_kind = parts + 3
    edge_start(kappa_kind)

    f32 = jnp.float32
    tall = r.u.shape[2]

    def blank(count):
        return jnp.zeros((count, width), f32)

    def clear_planes(ref):
        for n in range(ref.shape[0]):
            for plane in (0, nz + 1):
                ref[n, plane] = blank(tall)

    for ref in (r.u, r.c, r.cu, r.e1, r.ce1, r.e2, r.ce2, r.mc, r.me1, r.cme1, r.me2, r.cme2, r.tc, r.te, r.cte):
        clear_planes(ref)

    def clear_rows(p, carry):
        for ref in (r.u, r.c, r.cu, r.e1, r.ce1):
            for n in range(ref.shape[0]):
                ref[n, p + 1, pl.ds(0, halo), :] = blank(halo)
                ref[n, p + 1, pl.ds(tall - halo, halo), :] = blank(halo)
        for ref in (r.e2, r.ce2, r.mc, r.me1, r.cme1, r.me2, r.cme2, r.tc, r.te, r.cte):
            for n in range(ref.shape[0]):
                ref[n, p + 1, pl.ds(halo, halo), :] = blank(halo)
                ref[n, p + 1, pl.ds(tall - pad, halo), :] = blank(halo)
        return carry

    lax.fori_loop(0, nz, clear_rows, 0)
    strips = (r.su, r.sc, r.scu, r.se1, r.sce1, r.se2, r.sce2, r.smc, r.sme1, r.scme1, r.sme2, r.scme2, r.stc, r.ste, r.scte)
    for ref in strips:
        for n in range(ref.shape[0]):
            for side in range(2):
                ref[n, side] = blank(tall)
    if chained:

        @pl.when(jnp.logical_not(has_prev))
        def _():
            def clear_first(p, carry):
                for ref in (r.u, r.e1, r.e2, r.me1, r.me2, r.te):
                    ref[0, p + 1] = blank(tall)
                return carry

            lax.fori_loop(0, nz, clear_first, 0)

    for number, (has, _) in enumerate(flanks):
        edge = pl.ds((pad - halo, pad + tx)[number], halo)

        @pl.when(jnp.logical_not(has))
        def _():
            def clear_edges(p, carry):
                r.kap[p, edge, :] = blank(halo)
                for n in range(group):
                    r.u[n + 1, p + 1, edge, :] = blank(halo)
                    r.src[n, p, edge, :] = blank(halo)
                return carry

            lax.fori_loop(0, nz, clear_edges, 0)
            for side in range(2):
                r.kap_strip[side, edge, :] = blank(halo)
                for f in range(2):
                    for n in range(group):
                        r.strip_in[f, n, side, edge, :] = blank(halo)

    for side in range(2):

        @pl.when(jnp.logical_not(beside_has[side]))
        def _():
            def clear_beside(p, carry):
                r.beside[side, p] = blank(tx)
                return carry

            lax.fori_loop(0, nz, clear_beside, 0)

    lane_tx = lax.broadcasted_iota(jnp.int32, (tx, width), 1)
    lane = lax.broadcasted_iota(jnp.int32, (tx + 2 * halo, width), 1)

    def plane_of(side, lanes):
        return ((lanes + (span // 2, 0)[side]) % width) // span

    inside = [plane_of(side, lane_tx) for side in range(2)]

    def put_strip(packed, side, block, p):
        return jnp.where(inside[side] == p, pltpu.roll(block, span * p + 2, 1), packed)

    nothing = blank(tx)

    def pack_own(f):
        def body(p, packed):
            blocks = [r.own[f, p, :, d * width : (d + 1) * width] for d in range(group)]
            made = []
            for d in range(group):
                left, right = packed[2 * d], packed[2 * d + 1]
                turned_left = blocks[d - 1] if d else None
                turned_right = blocks[d + 1] if d < group - 1 else None
                made.append(left if turned_left is None else put_strip(left, 0, turned_left, p))
                made.append(right if turned_right is None else put_strip(right, 1, turned_right, p))
            return tuple(made)

        packed = lax.fori_loop(0, nz, body, (nothing,) * (2 * group), unroll=2)
        for d in range(group):
            for side in range(2):
                r.strip_send[f, d, side] = packed[2 * d + side]
        for side in range(2):
            r.strip_in[f, q, side, real, :] = r.strip_send[f, q, side]

    for f in range(2):
        own_copies[f].wait()
        pack_own(f)
        for j in order[:3]:
            strip_copy(f, j).start()
        for n in range(group):

            @pl.when(q == n)
            def _():
                edge_start(parts + 1 + f, n)

    for part in range(parts):
        for j in order:
            in_copy(1 + part, j).start()

    for side in range(2):

        @pl.when(beside_has[side])
        def _():
            beside_copy(side).wait()

    def kappa_body(p, packed):
        return tuple(put_strip(packed[side], side, r.beside[side, p], p) for side in range(2))

    packed = lax.fori_loop(0, nz, kappa_body, (nothing, nothing), unroll=2)
    for side in range(2):
        r.kap_strip[side, real, :] = packed[side]
    strip_kappa = parts + 4
    edge_start(strip_kappa)

    level = lax.broadcasted_iota(jnp.int32, (tx + 2 * halo, width), 0)
    below = jnp.where(has_dn, damping, 0.0)
    above = jnp.where(has_up, damping, 0.0)
    damp = jnp.where(level < halo, below, jnp.where(level < halo + tx, damping, above))
    r.damp[0, rows(full), :] = damp
    for side in range(2):
        r.damp[1 + side, rows(full), :] = damp * jnp.where(beside_has[side], 1.0, 0.0)

    first_plane = [plane_of(side, lane) == 0 for side in range(2)]
    last_plane = [plane_of(side, lane) == nz - 1 for side in range(2)]
    inject = [lane % span == 2, lane % span == 1]
    plane_lane = lane // span
    first_lane = lane == 0
    last_lane = lane == width - 1

    def cut(mask, win):
        return mask[: win[1]]

    def pack(packed, value, p, win):
        return jnp.where(cut(plane_lane, win) == p, pltpu.roll(value, span * p + 2, 1), packed)

    def ghosts(ref, n, win):
        left = pltpu.roll(ref[n, 0, rows(win), :], 1, 1)
        right = pltpu.roll(ref[n, 1, rows(win), :], width - 1, 1)
        return jnp.where(cut(inject[0], win), left, right)

    def sideways(value, ghost, p, win):
        edge = pltpu.roll(ghost, width - 2 - span * p, 1)
        left = jnp.where(cut(first_lane, win), edge, pltpu.roll(value, 1, 1))
        right = jnp.where(cut(last_lane, win), edge, pltpu.roll(value, width - 1, 1))
        return left, right

    def across(ref, n, p, win):
        return (
            (ref[n, p + 1, rows(win, -1), :] + ref[n, p + 1, rows(win, 1), :])
            + (ref[n, p, rows(win), :] + ref[n, p + 2, rows(win), :])
        )

    def planes_loop(body, init, first=0, count=None):
        count = nz if count is None else count
        return lax.fori_loop(first, first + count, body, init, unroll=unroll)

    def earlier(ref, n, middle, win):
        if n == 0 and not chained:
            return None
        return ref[n, middle, rows(win), :]

    def pull(v_ref, cv_ref, w, n, ghost, p, win, first):
        v = v_ref[first + n, p + 1, rows(win), :]
        left, right = sideways(v, ghost, p, win)
        total = w.l[n, p, rows(win), :] * left + w.r[n, p, rows(win), :] * right
        total = total + w.c[n, p + 1, rows(win), :] * across(v_ref, first + n, p, win)
        total = total + across(cv_ref, n, p, win)
        before = earlier(v_ref, n, p + 1, win)
        if before is not None:
            total = total + before
        return v, total - w.a[n, p, rows(win), :] * v

    def strip_pull(v_ref, cv_ref, w, n, side, win, first):
        v = v_ref[first + n, side, rows(win), :]
        total = w.sl[n, side, rows(win), :] * pltpu.roll(v, 1, 1)
        total = total + w.sr[n, side, rows(win), :] * pltpu.roll(v, width - 1, 1)
        total = total + w.sd[n, side, rows(win), :] * pltpu.roll(v, span, 1)
        total = total + w.su[n, side, rows(win), :] * pltpu.roll(v, width - span, 1)
        beside = v_ref[first + n, side, rows(win, -1), :] + v_ref[first + n, side, rows(win, 1), :]
        total = total + w.sc[n, side, rows(win), :] * beside
        total = total + (cv_ref[n, side, rows(win, -1), :] + cv_ref[n, side, rows(win, 1), :])
        before = earlier(v_ref, n, side, win)
        if before is not None:
            total = total + before
        return v, total - w.sa[n, side, rows(win), :] * v

    def put_values(v_ref, cv_ref, w, n, side, win, value, packed, first):
        value = jnp.where(cut(inject[side], win), packed, value)
        v_ref[first + n, side, rows(win), :] = value
        cv_ref[n, side, rows(win), :] = w.sc[n, side, rows(win), :] * value

    fine = types.SimpleNamespace(
        l=r.wl, r=r.wr, a=r.wa, c=r.c, d=r.rd, sl=r.swl, sr=r.swr, sd=r.swd, su=r.swu, sa=r.swa, sc=r.sc, sg=r.srd
    )
    mid = types.SimpleNamespace(
        l=r.mwl, r=r.mwr, a=r.mwa, c=r.mc, d=r.mrd, sl=r.smwl, sr=r.smwr, sd=r.smwd, su=r.smwu, sa=r.smwa,
        sc=r.smc, sg=r.smrd,
    )
    top = types.SimpleNamespace(
        l=r.twl, r=r.twr, a=r.twa, c=r.tc, d=r.trd, sl=r.stwl, sr=r.stwr, sd=r.stwd, su=r.stwu, sa=r.stwa,
        sc=r.stc, sg=r.strd,
    )

    wide = blank(full[1])
    edge_recv_wait(kappa_kind)
    edge_recv_wait(strip_kappa)
    kappa_edge = planes_loop(lambda p, packed: pack(packed, r.kap[p, rows(full), :], p, full), wide)

    def slices(body):
        for j in (0, 2, 1, 3):
            body(j)

    def arrived(copies, n_of, then):
        for j in (0,) + order[:3]:
            if j:
                copies(j).wait_recv()
            else:
                copies(j).wait()
        for n in range(group):
            then(n)

    arrived(lambda j: in_copy(0, j), None, lambda n: edge_start(0, n))
    for f in range(2):
        for j in order[:3]:
            strip_copy(f, j).wait_recv()
        for n in range(group):

            @pl.when(q != n)
            def _():
                edge_start(parts + 1 + f, n)

    for n in range(group):
        edge_recv_wait(0, n)
        edge_recv_wait(parts + 1, n)

        def body(p, packed):
            v = r.u[n + 1, p + 1, rows(full), :]
            cc = (half * r.kap[p, rows(full), :]) * (1.0 + v * v)
            r.c[n, p + 1, rows(full), :] = cc
            r.cu[n, p + 1, rows(full), :] = cc * v
            return pack(packed, v, p, full)

        packed = planes_loop(body, wide)
        for side in range(2):
            v = jnp.where(inject[side], packed, r.strip_in[0, n, side, rows(full), :])
            kk = jnp.where(inject[side], kappa_edge, r.kap_strip[side, rows(full), :])
            cc = (half * kk) * (1.0 + v * v)
            r.su[n + 1, side, rows(full), :] = v
            r.sc[n, side, rows(full), :] = cc
            r.scu[n, side, rows(full), :] = cc * v
    time_send(0)
    time_wait(0)

    for n in range(group):
        for side in range(2):
            cc = r.sc[n, side, rows(full), :]
            total = r.sc[n, side, rows(full, -1), :] + r.sc[n, side, rows(full, 1), :]
            for ref, shift, off in (
                (r.swl, 1, None), (r.swr, width - 1, None),
                (r.swd, span, first_plane[side]), (r.swu, width - span, last_plane[side]),
            ):
                near = pltpu.roll(cc, shift, 1)
                weight = cc + near
                if off is not None:
                    near, weight = jnp.where(off, 0.0, near), jnp.where(off, 0.0, weight)
                ref[n, side, rows(full), :] = weight
                total = total + near
            diagonal = 1.0 + (6.0 * cc + total)
            r.swa[n, side, rows(full), :] = diagonal
            r.srd[n, side, rows(full), :] = r.damp[1 + side, rows(full), :] / diagonal
        ghost_c, ghost_u = ghosts(r.sc, n, full), ghosts(r.su, n + 1, full)

        def body(p, carry):
            cc = r.c[n, p + 1, rows(full), :]
            left, right = sideways(cc, ghost_c, p, full)
            left, right = cc + left, cc + right
            r.wl[n, p, rows(full), :] = left
            r.wr[n, p, rows(full), :] = right
            diagonal = 1.0 + ((4.0 * cc + left) + (right + across(r.c, n, p, full)))
            r.wa[n, p, rows(full), :] = diagonal
            r.rd[n, p, rows(full), :] = r.damp[0, rows(full), :] / diagonal
            _, total = pull(r.u, r.cu, fine, n, ghost_u, p, full, 1)
            r.res[n, p, rows(full), :] = total
            return carry

        planes_loop(body, 0)
        for side in range(2):
            _, total = strip_pull(r.su, r.scu, fine, n, side, full, 1)
            r.sres[n, side, rows(full), :] = total

    pairs = ((mid, fine, 2), (top, mid, 1))
    for to, of, count in pairs:
        for n in range(count):

            def body(p, carry):
                to.c[n, p + 1, rows(full), :] = of.c[2 * n, p + 1, rows(full), :] + of.c[2 * n + 1, p + 1, rows(full), :]
                for one, two in ((to.l, of.l), (to.r, of.r)):
                    one[n, p, rows(full), :] = two[2 * n, p, rows(full), :] + two[2 * n + 1, p, rows(full), :]
                diagonal = (of.a[2 * n, p, rows(full), :] - 1.0) + of.a[2 * n + 1, p, rows(full), :]
                to.a[n, p, rows(full), :] = diagonal
                to.d[n, p, rows(full), :] = r.damp[0, rows(full), :] / diagonal
                return carry

            planes_loop(body, 0)
            for side in range(2):
                for one, two in (
                    (to.sc, of.sc), (to.sl, of.sl), (to.sr, of.sr), (to.sd, of.sd), (to.su, of.su),
                ):
                    one[n, side, rows(full), :] = two[2 * n, side, rows(full), :] + two[2 * n + 1, side, rows(full), :]
                diagonal = (of.sa[2 * n, side, rows(full), :] - 1.0) + of.sa[2 * n + 1, side, rows(full), :]
                to.sa[n, side, rows(full), :] = diagonal
                to.sg[n, side, rows(full), :] = r.damp[1 + side, rows(full), :] / diagonal

    for n in range(group):
        edge_recv_wait(parts + 2, n)

    def first_update(n, part, win, packed):
        def body(p, packed):
            left = r.src[n, p, rows(win), :] + r.res[n, p, rows(win), :]
            r.res[n, p, rows(win), :] = left
            update = left * r.rd[n, p, rows(win), :]
            r.e1[n + 1, p + 1, rows(win), :] = update
            r.ce1[n, p + 1, rows(win), :] = r.c[n, p + 1, rows(win), :] * update
            return pack(packed, update, p, win)

        return planes_loop(body, packed, part * piece, piece)

    outer = [(pad - halo, halo), (pad + tx, halo)]
    for part in range(parts):
        kind = 1 + part
        arrived(lambda j: in_copy(kind, j), None, lambda n: edge_start(kind, n))
        for n in range(group):
            packed = r.packed_one[n, rows(core), :] if part else nothing
            r.packed_one[n, rows(core), :] = first_update(n, part, core, packed)
        for j in order:
            out_copy(0, j, part).start()
        for n in range(group):
            edge_recv_wait(kind, n)
            for win in outer:
                packed = r.packed_one[n, rows(win), :] if part else blank(halo)
                r.packed_one[n, rows(win), :] = first_update(n, part, win, packed)
    for n in range(group):
        for side in range(2):
            left = r.strip_in[1, n, side, rows(full), :] + r.sres[n, side, rows(full), :]
            r.sres[n, side, rows(full), :] = left
            put_values(
                r.se1, r.sce1, fine, n, side, full, left * r.srd[n, side, rows(full), :],
                r.packed_one[n, rows(full), :], 1,
            )
    time_send(1)
    time_wait(1)

    narrow = blank(trim[1])

    def again(w, v, cv, sv, scv, b, sb, to_v, to_cv, to_sv, to_scv, count):
        for n in range(count):
            ghost = ghosts(sv, n + 1, trim)

            def body(p, packed):
                value, total = pull(v, cv, w, n, ghost, p, trim, 1)
                left = b[n, p, rows(trim), :] + total
                update = value + left * w.d[n, p, rows(trim), :]
                to_v[n + 1, p + 1, rows(trim), :] = update
                to_cv[n, p + 1, rows(trim), :] = w.c[n, p + 1, rows(trim), :] * update
                return pack(packed, update, p, trim)

            packed = planes_loop(body, narrow)
            for side in range(2):
                value, total = strip_pull(sv, scv, w, n, side, trim, 1)
                left = sb[n, side, rows(trim), :] + total
                update = value + left * w.sg[n, side, rows(trim), :]
                put_values(to_sv, to_scv, w, n, side, trim, update, packed, 1)

    def coarsen(w, to, v, cv, sv, scv, b, sb, to_b, to_sb, to_v, to_cv, to_sv, to_scv, count):
        for n in range(count):
            pair = [ghosts(sv, 2 * n + i + 1, trim) for i in range(2)]

            def body(p, packed):
                rhs = None
                for i in range(2):
                    _, total = pull(v, cv, w, 2 * n + i, pair[i], p, trim, 1)
                    left = b[2 * n + i, p, rows(trim), :] + total
                    rhs = left if rhs is None else rhs + left
                to_b[n, p, rows(trim), :] = rhs
                update = rhs * to.d[n, p, rows(trim), :]
                to_v[n + 1, p + 1, rows(trim), :] = update
                to_cv[n, p + 1, rows(trim), :] = to.c[n, p + 1, rows(trim), :] * update
                return pack(packed, update, p, trim)

            packed = planes_loop(body, narrow)
            for side in range(2):
                rhs = None
                for i in range(2):
                    _, total = strip_pull(sv, scv, w, 2 * n + i, side, trim, 1)
                    left = sb[2 * n + i, side, rows(trim), :] + total
                    rhs = left if rhs is None else rhs + left
                to_sb[n, side, rows(trim), :] = rhs
                update = rhs * to.sg[n, side, rows(trim), :]
                put_values(to_sv, to_scv, to, n, side, trim, update, packed, 1)

    again(fine, r.e1, r.ce1, r.se1, r.sce1, r.res, r.sres, r.e2, r.ce2, r.se2, r.sce2, group)
    time_send(2)
    time_wait(2)
    coarsen(
        fine, mid, r.e2, r.ce2, r.se2, r.sce2, r.res, r.sres, r.mb, r.smb, r.me1, r.cme1, r.sme1, r.scme1, 2
    )
    time_send(3)
    time_wait(3)
    again(mid, r.me1, r.cme1, r.sme1, r.scme1, r.mb, r.smb, r.me2, r.cme2, r.sme2, r.scme2, 2)
    time_send(4)
    time_wait(4)
    coarsen(
        mid, top, r.me2, r.cme2, r.sme2, r.scme2, r.mb, r.smb, r.tb, r.stb, r.te, r.cte, r.ste, r.scte, 1
    )
    time_send(5)
    time_wait(5)
    ghost = ghosts(r.ste, 1, core)

    def body(p, carry):
        value, total = pull(r.te, r.cte, top, 0, ghost, p, core, 1)
        update = value + (r.tb[0, p, real, :] + total) * r.trd[0, p, real, :]
        for n in range(group):
            middle = r.me2[n // 2 + 1, p + 1, real, :] + update
            r.new[n, p, real, :] = r.u[n + 1, p + 1, real, :] + (r.e2[n + 1, p + 1, real, :] + middle)
        return carry

    for part in range(parts):
        planes_loop(body, 0, part * piece, piece)
        for j in order:
            out_copy(1, j, part).start()

    for f in range(2):
        for j in order[:3]:
            strip_copy(f, j).wait_send()
    for a in range(1 + parts):
        for j in order[:3]:
            in_copy(a, j).wait_send()
    for kind in range(parts + 3):
        for n in range(group):
            edge_wait(kind, n, True)
    edge_wait(kappa_kind, 0, True)
    edge_wait(strip_kappa, 0, True)
    if chained:

        @pl.when(has_next)
        def _():
            for number in range(len(time_refs)):
                for copy in time_copies(number):
                    copy.wait_send()

    for a in range(2):
        for part in range(parts):
            for j in order:
                if j == 0:
                    out_copy(a, j, part).wait()
                else:
                    out_copy(a, j, part).wait_send()
                    out_copy(a, j, part).wait_recv()


def shards(tm_size, space_size, iterate, source_term, conductivity):
    _, nz, tx, ty = conductivity.shape
    width = ty // group
    tall = tx + 2 * pad
    f32 = jnp.float32
    dma = pltpu.SemaphoreType.DMA
    kinds = parts + 5

    def padded(count):
        return pltpu.VMEM((count, nz + 2, tall, width), f32)

    def plain(*lead):
        return pltpu.VMEM((*lead, nz, tall, width), f32)

    def strip(*lead):
        return pltpu.VMEM((*lead, 2, tall, width), f32)

    scratch = {"packed": pltpu.VMEM((1, nz, 8, width), f32)}
    scratch |= {name: padded(count) for name, count in (
        ("u", 5), ("c", 4), ("cu", 4), ("e1", 5), ("ce1", 4), ("e2", 5), ("ce2", 4), ("mc", 2), ("me1", 3),
        ("cme1", 2), ("me2", 3), ("cme2", 2), ("tc", 1), ("te", 2), ("cte", 1),
    )}
    scratch |= {name: plain(count) for name, count in (
        ("src", 4), ("res", 4), ("wl", 4), ("wr", 4), ("wa", 4), ("rd", 4), ("mwl", 2), ("mwr", 2), ("mwa", 2),
        ("mrd", 2), ("mb", 2), ("twl", 1), ("twr", 1), ("twa", 1), ("trd", 1), ("tb", 1), ("new", 4),
    )}
    scratch["kap"] = plain()
    scratch |= {name: strip(count) for name, count in (
        ("su", 5), ("sc", 4), ("scu", 4), ("se1", 5), ("sce1", 4), ("se2", 5), ("sce2", 4), ("smc", 2),
        ("sme1", 3), ("scme1", 2), ("sme2", 3), ("scme2", 2), ("stc", 1), ("ste", 2), ("scte", 1),
        ("swl", 4), ("swr", 4), ("swd", 4), ("swu", 4), ("swa", 4), ("srd", 4), ("sres", 4),
        ("smwl", 2), ("smwr", 2), ("smwd", 2), ("smwu", 2), ("smwa", 2), ("smrd", 2), ("smb", 2),
        ("stwl", 1), ("stwr", 1), ("stwd", 1), ("stwu", 1), ("stwa", 1), ("strd", 1), ("stb", 1),
    )}
    scratch["kap_strip"] = strip()
    scratch["strip_in"] = strip(2, group)
    scratch["strip_send"] = pltpu.VMEM((2, group, 2, tx, width), f32)
    scratch["own"] = pltpu.VMEM((2, nz, tx, ty), f32)
    scratch["beside"] = pltpu.VMEM((2, nz, tx, width), f32)
    scratch["packed_one"] = pltpu.VMEM((group, tall, width), f32)
    scratch["damp"] = pltpu.VMEM((3, tall, width), f32)
    for name, shape in (
        ("loc_sem", (5,)), ("in_lsem", (1 + parts,)), ("in_ssem", (1 + parts, group - 1)),
        ("in_rsem", (1 + parts, group - 1)), ("out_lsem", (2, parts)), ("out_ssem", (2, parts, group - 1)),
        ("out_rsem", (2, parts, group - 1)), ("strip_ssem", (2, group - 1)), ("strip_rsem", (2, group - 1)),
        ("edge_ssem", (kinds, group, 2)), ("edge_rsem", (kinds, group, 2)), ("time_ssem", (6, 2)),
        ("time_rsem", (6, 2)),
    ):
        scratch[name] = dma(shape)
    names = ("state_in", "source_in", "kappa_in", "new_out", "res_out", *scratch)
    out = jax.ShapeDtypeStruct(iterate.shape, f32)
    hbm = pl.BlockSpec(memory_space=pltpu.HBM)
    return pl.pallas_call(
        functools.partial(kernel, tm_size, space_size, names),
        out_shape=(out, out),
        in_specs=[hbm] * 3,
        out_specs=(hbm, hbm),
        scratch_shapes=list(scratch.values()),
        compiler_params=pltpu.CompilerParams(
            collective_id=0, has_side_effects=True, vmem_limit_bytes=67043328
        ),
    )(iterate, source_term, conductivity)


def solution(mesh):
    tiled = P("tm", "space", None, None, None)
    in_specs = (tiled, tiled, P("space", None, None, None))
    body = functools.partial(shards, mesh.shape["tm"], mesh.shape["space"])
    return jax.shard_map(
        body, mesh=mesh, in_specs=in_specs, out_specs=(tiled, tiled), check_vma=False
    )
```

time: 65.7 us -> 67.5 us (1.027); the launches traced: 64.4 us -> 67.3 us
  Pallas kernels: 61 us -> 63.9 us
    pallas_call x1, Pallas kernels: 61 us -> 63.9 us  [shards(): pl.pallas_call(functools.partial(kernel, tm_size, space_size, names), out...]
where the time goes in v1:
time: 67.5 us; the launch traced here: 67.3 us
  Pallas kernels  63.9 us (95%)
  local copies, waits for them, and re-layouts  2.74 us (4%)
    pallas_call x1, Pallas kernels, shards(): pl.pallas_call(functools.partial(kernel, tm_size, space_size, names), out...  63.9 us
    unnamed x4, local copies, waits for them, and re-layouts  2.74 us

profile of v1, /device:TPU:5, one launch (start us, length us, event | category | flops | bytes accessed | tf_op | source)
XLA Modules:
  0.0 67.3 jit_solution(7253927803895149977)
XLA Ops:
  0.6 63.9 %shard_map.50 = (f32[1,1,16,16,512]{4,3,2,1,0:T(8,128)}, f32[1,1,16,16,512]{4,3,2,1,0:T(8,128)}) custom-call(f32[1,1,16,16,512]{4,3,2,1,0:T(8,128)} %refs_0_.1, f32[1,1,16,16,512]{4,3,2,1,0:T(8,128)} %refs_1_.1, f32[1,16,16,512]{3,2,1,0:T(8,128)} %refs_2_.1), custom_call_target="tpu_custom_call" | custom-call | tf_op jit(solution)/shard_map/pallas_call | solution.py:747
  64.6 0.0 copy-start
  64.6 1.9 %copy.7 = f32[1,1,16,16,512]{4,3,2,1,0:T(8,128)} copy(f32[1,1,16,16,512]{4,3,2,1,0:T(8,128)} %get-tuple-element.4) | data formatting | bytes 1048576
  66.5 0.0 copy-done
  66.5 0.8 %copy.8 = f32[1,1,16,16,512]{4,3,2,1,0:T(8,128)} copy(f32[1,1,16,16,512]{4,3,2,1,0:T(8,128)S(1)} %copy-done) | data formatting | bytes 1048576
Async XLA Ops:
  64.6 2.0 %copy-start = (f32[1,1,16,16,512]{4,3,2,1,0:T(8,128)S(1)}, f32[1,1,16,16,512]{4,3,2,1,0:T(8,128)}, u32[]{:S(2)}) copy-start(f32[1,1,16,16,512]{4,3,2,1,0:T(8,128)} %get-tuple-element.5) | copy-start | bytes 1572868

commit v2 on v1

--- a/solution.py
+++ b/solution.py
@@ -13,20 +13,21 @@
 group = 4
 halo = 8
 pad = 2 * halo
-parts = 2
+parts = 4
+out_parts = 2
 mesh_ids = pl.DeviceIdType.MESH
 order = (2, 1, 3, 0)
-unroll = 4
+unroll = 8
 
 
 def kernel(tm_size, space_size, names, *refs):
     r = types.SimpleNamespace(**dict(zip(names, refs)))
-    nz, _, width = r.packed.shape[1], None, r.kap.shape[-1]
-    tx = r.state_in.shape[3]
+    _, nz, tx, _ = r.kappa_in.shape
+    width = r.kap.shape[-1]
     span = width // nz
     chained = tm_size > group
     half = 0.5 * tau_step
-    piece = nz // parts
+    piece, out_piece = nz // parts, nz // out_parts
 
     full = (pad - halo, tx + 2 * halo)
     trim = (pad - halo // 2, tx + halo)
@@ -107,7 +108,7 @@
 
     def out_copy(a, j, part):
         d = (q + j) % group
-        some = pl.ds(part * piece, piece)
+        some = pl.ds(part * out_piece, out_piece)
         hbm = (r.res_out, r.new_out)[a].at[0, 0, some, :, columns(q)]
         held = (r.res, r.new)[a].at[d, some, real, :]
         if j == 0:
@@ -155,15 +156,12 @@
             def _():
                 edge_copy(kind, n, number).start()
 
-    def edge_wait(kind, n=0, send=False):
+    def edge_send_wait(kind, n=0):
         for number in range(2):
 
             @pl.when(flanks[number][0])
             def _():
-                if send:
-                    edge_copy(kind, n, number).wait_send()
-                else:
-                    edge_copy(kind, n, 1 - number).wait_recv()
+                edge_copy(kind, n, number).wait_send()
 
     def edge_recv_wait(kind, n=0):
         for number in range(2):
@@ -219,61 +217,6 @@
     def blank(count):
         return jnp.zeros((count, width), f32)
 
-    def clear_planes(ref):
-        for n in range(ref.shape[0]):
-            for plane in (0, nz + 1):
-                ref[n, plane] = blank(tall)
-
-    for ref in (r.u, r.c, r.cu, r.e1, r.ce1, r.e2, r.ce2, r.mc, r.me1, r.cme1, r.me2, r.cme2, r.tc, r.te, r.cte):
-        clear_planes(ref)
-
-    def clear_rows(p, carry):
-        for ref in (r.u, r.c, r.cu, r.e1, r.ce1):
-            for n in range(ref.shape[0]):
-                ref[n, p + 1, pl.ds(0, halo), :] = blank(halo)
-                ref[n, p + 1, pl.ds(tall - halo, halo), :] = blank(halo)
-        for ref in (r.e2, r.ce2, r.mc, r.me1, r.cme1, r.me2, r.cme2, r.tc, r.te, r.cte):
-            for n in range(ref.shape[0]):
-                ref[n, p + 1, pl.ds(halo, halo), :] = blank(halo)
-                ref[n, p + 1, pl.ds(tall - pad, halo), :] = blank(halo)
-        return carry
-
-    lax.fori_loop(0, nz, clear_rows, 0)
-    strips = (r.su, r.sc, r.scu, r.se1, r.sce1, r.se2, r.sce2, r.smc, r.sme1, r.scme1, r.sme2, r.scme2, r.stc, r.ste, r.scte)
-    for ref in strips:
-        for n in range(ref.shape[0]):
-            for side in range(2):
-                ref[n, side] = blank(tall)
-    if chained:
-
-        @pl.when(jnp.logical_not(has_prev))
-        def _():
-            def clear_first(p, carry):
-                for ref in (r.u, r.e1, r.e2, r.me1, r.me2, r.te):
-                    ref[0, p + 1] = blank(tall)
-                return carry
-
-            lax.fori_loop(0, nz, clear_first, 0)
-
-    for number, (has, _) in enumerate(flanks):
-        edge = pl.ds((pad - halo, pad + tx)[number], halo)
-
-        @pl.when(jnp.logical_not(has))
-        def _():
-            def clear_edges(p, carry):
-                r.kap[p, edge, :] = blank(halo)
-                for n in range(group):
-                    r.u[n + 1, p + 1, edge, :] = blank(halo)
-                    r.src[n, p, edge, :] = blank(halo)
-                return carry
-
-            lax.fori_loop(0, nz, clear_edges, 0)
-            for side in range(2):
-                r.kap_strip[side, edge, :] = blank(halo)
-                for f in range(2):
-                    for n in range(group):
-                        r.strip_in[f, n, side, edge, :] = blank(halo)
-
     for side in range(2):
 
         @pl.when(jnp.logical_not(beside_has[side]))
@@ -331,6 +274,63 @@
         for j in order:
             in_copy(1 + part, j).start()
 
+    held = [(ref, 1) for ref, _ in time_refs]
+    held += [(ref, 0) for ref in (r.c, r.cu, r.ce1, r.ce2, r.mc, r.cme1, r.cme2, r.tc, r.cte)]
+    early = (r.u, r.c, r.cu, r.e1, r.ce1)
+    for ref, first in held:
+        for n in range(first, ref.shape[0]):
+            for plane in (0, nz + 1):
+                ref[n, plane] = blank(tall)
+
+    def clear_rows(p, carry):
+        for ref, first in held:
+            outer = any(ref is one for one in early)
+            low, high = (0, tall - halo) if outer else (halo, tall - pad)
+            for n in range(first, ref.shape[0]):
+                ref[n, p + 1, pl.ds(low, halo), :] = blank(halo)
+                ref[n, p + 1, pl.ds(high, halo), :] = blank(halo)
+        return carry
+
+    lax.fori_loop(0, nz, clear_rows, 0)
+    strips = [(ref, 1) for ref, _ in time_strips]
+    strips += [(ref, 0) for ref in (r.sc, r.scu, r.sce1, r.sce2, r.smc, r.scme1, r.scme2, r.stc, r.scte)]
+    for ref, first in strips:
+        for n in range(first, ref.shape[0]):
+            for side in range(2):
+                ref[n, side] = blank(tall)
+    if chained:
+
+        @pl.when(jnp.logical_not(has_prev))
+        def _():
+            def clear_first(p, carry):
+                for ref, _ in time_refs:
+                    ref[0, p + 1] = blank(tall)
+                return carry
+
+            lax.fori_loop(0, nz, clear_first, 0)
+            for ref, _ in time_strips:
+                for side in range(2):
+                    ref[0, side] = blank(tall)
+
+    for number, (has, _) in enumerate(flanks):
+        edge = pl.ds((pad - halo, pad + tx)[number], halo)
+
+        @pl.when(jnp.logical_not(has))
+        def _():
+            def clear_edges(p, carry):
+                r.kap[p, edge, :] = blank(halo)
+                for n in range(group):
+                    r.u[n + 1, p + 1, edge, :] = blank(halo)
+                    r.src[n, p, edge, :] = blank(halo)
+                return carry
+
+            lax.fori_loop(0, nz, clear_edges, 0)
+            for side in range(2):
+                r.kap_strip[side, edge, :] = blank(halo)
+                for f in range(2):
+                    for n in range(group):
+                        r.strip_in[f, n, side, edge, :] = blank(halo)
+
     for side in range(2):
 
         @pl.when(beside_has[side])
@@ -367,6 +367,12 @@
     def pack(packed, value, p, win):
         return jnp.where(cut(plane_lane, win) == p, pltpu.roll(value, span * p + 2, 1), packed)
 
+    def pack_planes(ref, n, win, packed, first=0, count=None):
+        def body(p, packed):
+            return pack(packed, ref[n, p + 1, rows(win), :], p, win)
+
+        return planes_loop(body, packed, first, count)
+
     def ghosts(ref, n, win):
         left = pltpu.roll(ref[n, 0, rows(win), :], 1, 1)
         right = pltpu.roll(ref[n, 1, rows(win), :], width - 1, 1)
@@ -386,7 +392,7 @@
 
     def planes_loop(body, init, first=0, count=None):
         count = nz if count is None else count
-        return lax.fori_loop(first, first + count, body, init, unroll=unroll)
+        return lax.fori_loop(first, first + count, body, init, unroll=min(unroll, count))
 
     def earlier(ref, n, middle, win):
         if n == 0 and not chained:
@@ -440,20 +446,14 @@
     edge_recv_wait(strip_kappa)
     kappa_edge = planes_loop(lambda p, packed: pack(packed, r.kap[p, rows(full), :], p, full), wide)
 
-    def slices(body):
-        for j in (0, 2, 1, 3):
-            body(j)
-
-    def arrived(copies, n_of, then):
-        for j in (0,) + order[:3]:
-            if j:
-                copies(j).wait_recv()
-            else:
-                copies(j).wait()
+    def arrived(a):
+        in_copy(a, 0).wait()
+        for j in order[:3]:
+            in_copy(a, j).wait_recv()
         for n in range(group):
-            then(n)
-
-    arrived(lambda j: in_copy(0, j), None, lambda n: edge_start(0, n))
+            edge_start(a, n)
+
+    arrived(0)
     for f in range(2):
         for j in order[:3]:
             strip_copy(f, j).wait_recv()
@@ -467,14 +467,15 @@
         edge_recv_wait(0, n)
         edge_recv_wait(parts + 1, n)
 
-        def body(p, packed):
+        def body(p, carry):
             v = r.u[n + 1, p + 1, rows(full), :]
             cc = (half * r.kap[p, rows(full), :]) * (1.0 + v * v)
             r.c[n, p + 1, rows(full), :] = cc
             r.cu[n, p + 1, rows(full), :] = cc * v
-            return pack(packed, v, p, full)
-
-        packed = planes_loop(body, wide)
+            return carry
+
+        planes_loop(body, 0)
+        packed = pack_planes(r.u, n + 1, full, wide)
         for side in range(2):
             v = jnp.where(inject[side], packed, r.strip_in[0, n, side, rows(full), :])
             kk = jnp.where(inject[side], kappa_edge, r.kap_strip[side, rows(full), :])
@@ -521,6 +522,9 @@
         for side in range(2):
             _, total = strip_pull(r.su, r.scu, fine, n, side, full, 1)
             r.sres[n, side, rows(full), :] = total
+        if n == 1:
+            arrived(1)
+    arrived(2)
 
     pairs = ((mid, fine, 2), (top, mid, 1))
     for to, of, count in pairs:
@@ -548,31 +552,41 @@
     for n in range(group):
         edge_recv_wait(parts + 2, n)
 
-    def first_update(n, part, win, packed):
-        def body(p, packed):
+    def first_update(n, part, win):
+        def body(p, carry):
             left = r.src[n, p, rows(win), :] + r.res[n, p, rows(win), :]
             r.res[n, p, rows(win), :] = left
             update = left * r.rd[n, p, rows(win), :]
             r.e1[n + 1, p + 1, rows(win), :] = update
             r.ce1[n, p + 1, rows(win), :] = r.c[n, p + 1, rows(win), :] * update
-            return pack(packed, update, p, win)
-
-        return planes_loop(body, packed, part * piece, piece)
+            return carry
+
+        planes_loop(body, 0, part * piece, piece)
 
     outer = [(pad - halo, halo), (pad + tx, halo)]
+
+    def inner_update(part):
+        for n in range(group):
+            first_update(n, part, core)
+        if (part + 1) * piece % out_piece == 0:
+            for j in order:
+                out_copy(0, j, (part + 1) * piece // out_piece - 1).start()
+
+    def outer_update(part):
+        for n in range(group):
+            edge_recv_wait(1 + part, n)
+            for win in outer:
+                first_update(n, part, win)
+            packed = r.packed_one[n, rows(full), :] if part else wide
+            r.packed_one[n, rows(full), :] = pack_planes(r.e1, n + 1, full, packed, part * piece, piece)
+
     for part in range(parts):
-        kind = 1 + part
-        arrived(lambda j: in_copy(kind, j), None, lambda n: edge_start(kind, n))
-        for n in range(group):
-            packed = r.packed_one[n, rows(core), :] if part else nothing
-            r.packed_one[n, rows(core), :] = first_update(n, part, core, packed)
-        for j in order:
-            out_copy(0, j, part).start()
-        for n in range(group):
-            edge_recv_wait(kind, n)
-            for win in outer:
-                packed = r.packed_one[n, rows(win), :] if part else blank(halo)
-                r.packed_one[n, rows(win), :] = first_update(n, part, win, packed)
+        if part > 1:
+            arrived(1 + part)
+        inner_update(part)
+        if part:
+            outer_update(part - 1)
+    outer_update(parts - 1)
     for n in range(group):
         for side in range(2):
             left = r.strip_in[1, n, side, rows(full), :] + r.sres[n, side, rows(full), :]
@@ -590,15 +604,16 @@
         for n in range(count):
             ghost = ghosts(sv, n + 1, trim)
 
-            def body(p, packed):
+            def body(p, carry):
                 value, total = pull(v, cv, w, n, ghost, p, trim, 1)
                 left = b[n, p, rows(trim), :] + total
                 update = value + left * w.d[n, p, rows(trim), :]
                 to_v[n + 1, p + 1, rows(trim), :] = update
                 to_cv[n, p + 1, rows(trim), :] = w.c[n, p + 1, rows(trim), :] * update
-                return pack(packed, update, p, trim)
-
-            packed = planes_loop(body, narrow)
+                return carry
+
+            planes_loop(body, 0)
+            packed = pack_planes(to_v, n + 1, trim, narrow)
             for side in range(2):
                 value, total = strip_pull(sv, scv, w, n, side, trim, 1)
                 left = sb[n, side, rows(trim), :] + total
@@ -609,7 +624,7 @@
         for n in range(count):
             pair = [ghosts(sv, 2 * n + i + 1, trim) for i in range(2)]
 
-            def body(p, packed):
+            def body(p, carry):
                 rhs = None
                 for i in range(2):
                     _, total = pull(v, cv, w, 2 * n + i, pair[i], p, trim, 1)
@@ -619,9 +634,10 @@
                 update = rhs * to.d[n, p, rows(trim), :]
                 to_v[n + 1, p + 1, rows(trim), :] = update
                 to_cv[n, p + 1, rows(trim), :] = to.c[n, p + 1, rows(trim), :] * update
-                return pack(packed, update, p, trim)
-
-            packed = planes_loop(body, narrow)
+                return carry
+
+            planes_loop(body, 0)
+            packed = pack_planes(to_v, n + 1, trim, narrow)
             for side in range(2):
                 rhs = None
                 for i in range(2):
@@ -658,8 +674,8 @@
             r.new[n, p, real, :] = r.u[n + 1, p + 1, real, :] + (r.e2[n + 1, p + 1, real, :] + middle)
         return carry
 
-    for part in range(parts):
-        planes_loop(body, 0, part * piece, piece)
+    for part in range(out_parts):
+        planes_loop(body, 0, part * out_piece, out_piece)
         for j in order:
             out_copy(1, j, part).start()
 
@@ -671,9 +687,9 @@
             in_copy(a, j).wait_send()
     for kind in range(parts + 3):
         for n in range(group):
-            edge_wait(kind, n, True)
-    edge_wait(kappa_kind, 0, True)
-    edge_wait(strip_kappa, 0, True)
+            edge_send_wait(kind, n)
+    edge_send_wait(kappa_kind)
+    edge_send_wait(strip_kappa)
     if chained:
 
         @pl.when(has_next)
@@ -683,7 +699,7 @@
                     copy.wait_send()
 
     for a in range(2):
-        for part in range(parts):
+        for part in range(out_parts):
             for j in order:
                 if j == 0:
                     out_copy(a, j, part).wait()
@@ -709,7 +725,7 @@
     def strip(*lead):
         return pltpu.VMEM((*lead, 2, tall, width), f32)
 
-    scratch = {"packed": pltpu.VMEM((1, nz, 8, width), f32)}
+    scratch = {}
     scratch |= {name: padded(count) for name, count in (
         ("u", 5), ("c", 4), ("cu", 4), ("e1", 5), ("ce1", 4), ("e2", 5), ("ce2", 4), ("mc", 2), ("me1", 3),
         ("cme1", 2), ("me2", 3), ("cme2", 2), ("tc", 1), ("te", 2), ("cte", 1),
@@ -735,8 +751,8 @@
     scratch["damp"] = pltpu.VMEM((3, tall, width), f32)
     for name, shape in (
         ("loc_sem", (5,)), ("in_lsem", (1 + parts,)), ("in_ssem", (1 + parts, group - 1)),
-        ("in_rsem", (1 + parts, group - 1)), ("out_lsem", (2, parts)), ("out_ssem", (2, parts, group - 1)),
-        ("out_rsem", (2, parts, group - 1)), ("strip_ssem", (2, group - 1)), ("strip_rsem", (2, group - 1)),
+        ("in_rsem", (1 + parts, group - 1)), ("out_lsem", (2, out_parts)), ("out_ssem", (2, out_parts, group - 1)),
+        ("out_rsem", (2, out_parts, group - 1)), ("strip_ssem", (2, group - 1)), ("strip_rsem", (2, group - 1)),
         ("edge_ssem", (kinds, group, 2)), ("edge_rsem", (kinds, group, 2)), ("time_ssem", (6, 2)),
         ("time_rsem", (6, 2)),
     ):

time: 67.5 us -> 61.9 us (0.917)
  Pallas kernels: 63.9 us -> 58 us
    pallas_call x1, Pallas kernels: 63.9 us -> 58 us  [shards(): pl.pallas_call(functools.partial(kernel, tm_size, space_size, names), out...]
where the time goes in v2:
time: 61.9 us; the launch traced here: 61.4 us
  Pallas kernels  58 us (94%)
  local copies, waits for them, and re-layouts  2.74 us (4%)
  between operations  0.65 us (1%)
    pallas_call x1, Pallas kernels, shards(): pl.pallas_call(functools.partial(kernel, tm_size, space_size, names), out...  58 us
    unnamed x4, local copies, waits for them, and re-layouts  2.74 us

profile of v2, /device:TPU:5, one launch (start us, length us, event | category | flops | bytes accessed | tf_op | source)
XLA Modules:
  0.0 61.4 jit_solution(9685666888395710453)
XLA Ops:
  0.6 58.0 %shard_map.50 = (f32[1,1,16,16,512]{4,3,2,1,0:T(8,128)}, f32[1,1,16,16,512]{4,3,2,1,0:T(8,128)}) custom-call(f32[1,1,16,16,512]{4,3,2,1,0:T(8,128)} %refs_0_.1, f32[1,1,16,16,512]{4,3,2,1,0:T(8,128)} %refs_1_.1, f32[1,16,16,512]{3,2,1,0:T(8,128)} %refs_2_.1), custom_call_target="tpu_custom_call" | custom-call | tf_op jit(solution)/shard_map/pallas_call | solution.py:763
  58.6 0.0 copy-start
  58.7 1.9 %copy.7 = f32[1,1,16,16,512]{4,3,2,1,0:T(8,128)} copy(f32[1,1,16,16,512]{4,3,2,1,0:T(8,128)} %get-tuple-element.4) | data formatting | bytes 1048576
  60.6 0.0 copy-done
  60.6 0.8 %copy.8 = f32[1,1,16,16,512]{4,3,2,1,0:T(8,128)} copy(f32[1,1,16,16,512]{4,3,2,1,0:T(8,128)S(1)} %copy-done) | data formatting | bytes 1048576
Async XLA Ops:
  58.6 2.0 %copy-start = (f32[1,1,16,16,512]{4,3,2,1,0:T(8,128)S(1)}, f32[1,1,16,16,512]{4,3,2,1,0:T(8,128)}, u32[]{:S(2)}) copy-start(f32[1,1,16,16,512]{4,3,2,1,0:T(8,128)} %get-tuple-element.5) | copy-start | bytes 1572868

commit v3 on v2

--- a/solution.py
+++ b/solution.py
@@ -13,6 +13,7 @@
 group = 4
 halo = 8
 pad = 2 * halo
+u_parts = 2
 parts = 4
 out_parts = 2
 mesh_ids = pl.DeviceIdType.MESH
@@ -27,7 +28,7 @@
     span = width // nz
     chained = tm_size > group
     half = 0.5 * tau_step
-    piece, out_piece = nz // parts, nz // out_parts
+    piece, u_piece, out_piece = nz // parts, nz // u_parts, nz // out_parts
 
     full = (pad - halo, tx + 2 * halo)
     trim = (pad - halo // 2, tx + halo)
@@ -45,6 +46,13 @@
     has_dn, has_up = sp > 0, sp < space_size - 1
     has_left, has_right = q > 0, q < group - 1
     has_prev, has_next = base > 0, base + group < tm_size
+    pair = group // 2
+    lower = q < pair
+    own_work = q != pair
+    far_block = jnp.where(lower, pair, 0)
+    near_block = jnp.where(lower, pair - 1, 0)
+    has_before = jnp.logical_and(own_work, me > 0)
+    has_after = jnp.logical_and(q != pair - 1, me + 1 < tm_size)
     flanks = [(has_dn, {"space": sp - 1}), (has_up, {"space": sp + 1})]
     beside_has = [has_left, has_right]
 
@@ -72,6 +80,45 @@
             beside_copy(side).start()
 
     own_copies[1].start()
+
+    def wide_columns(first, count):
+        return pl.ds(pl.multiple_of(first * width, width), count * width)
+
+    def far_copies():
+        made = []
+        for k in range(pair + 1):
+            made.append(
+                pltpu.make_async_copy(
+                    r.state_in.at[0, 0, :, :, columns(near_block + k)],
+                    r.lu.at[1 + k, pl.ds(1, nz), pl.ds(halo, tx), :], r.far_sem.at[0, k],
+                )
+            )
+            made.append(
+                pltpu.make_async_copy(
+                    r.kappa_in.at[0, :, :, columns(near_block + k)], r.lkap.at[1 + k], r.far_sem.at[1, k]
+                )
+            )
+        return made
+
+    @pl.when(own_work)
+    def _():
+        for copy in far_copies():
+            copy.start()
+
+    def before_copy():
+        first = jnp.where((q + 1) % group < pair, pair, 0)
+        return pltpu.make_async_remote_copy(
+            src_ref=r.state_in.at[0, 0, :, :, wide_columns(first, pair)], dst_ref=r.before,
+            send_sem=r.before_sem.at[0], recv_sem=r.before_sem.at[1], device_id={"tm": me + 1},
+            device_id_type=mesh_ids,
+        )
+
+    def row_copy(number):
+        return pltpu.make_async_remote_copy(
+            src_ref=r.row_send.at[number], dst_ref=r.row_in.at[1 - number],
+            send_sem=r.row_sem.at[0, number], recv_sem=r.row_sem.at[1, 1 - number],
+            device_id=flanks[number][1], device_id_type=mesh_ids,
+        )
 
     barrier = pltpu.get_barrier_semaphore()
     for j in range(1, group):
@@ -81,6 +128,8 @@
     greeted = list(flanks)
     if chained:
         greeted += [(has_prev, {"tm": me - group}), (has_next, {"tm": me + group})]
+        greeted += [(jnp.logical_and(has_prev, q == 0), {"tm": me - 1})]
+        greeted += [(jnp.logical_and(has_next, q == group - 1), {"tm": me + 1})]
     for has, where in greeted:
 
         @pl.when(has)
@@ -94,10 +143,12 @@
 
     def in_copy(a, j):
         d = (q + j) % group
-        if a == 0:
-            hbm, dst = r.state_in.at[0, 0, :, :, columns(d)], r.u.at[q + 1, planes, real, :]
+        if a < u_parts:
+            some = pl.ds(a * u_piece, u_piece)
+            hbm = r.state_in.at[0, 0, some, :, columns(d)]
+            dst = r.u.at[q + 1, pl.ds(1 + a * u_piece, u_piece), real, :]
         else:
-            some = pl.ds((a - 1) * piece, piece)
+            some = pl.ds((a - u_parts) * piece, piece)
             hbm, dst = r.source_in.at[0, 0, some, :, columns(d)], r.src.at[q, some, real, :]
         if j == 0:
             return pltpu.make_async_copy(hbm, dst, r.in_lsem.at[a])
@@ -119,56 +170,81 @@
             device_id_type=mesh_ids,
         )
 
-    def strip_copy(f, j):
+    def out_each(a, part, receiving, act):
+        for j in order[:3]:
+            one, two = ((q - j) % group, q) if receiving else (q, (q + j) % group)
+            if a == 0:
+                wanted = jnp.logical_or(one // pair == two // pair, jnp.logical_and(two == pair, one < pair))
+
+                @pl.when(wanted)
+                def _():
+                    act(out_copy(a, j, part))
+            else:
+                act(out_copy(a, j, part))
+
+    def strip_copy(j, side):
         d = (q + j) % group
         return pltpu.make_async_remote_copy(
-            src_ref=r.strip_send.at[f, d], dst_ref=r.strip_in.at[f, q, :, real, :],
-            send_sem=r.strip_ssem.at[f, j - 1], recv_sem=r.strip_rsem.at[f, j - 1],
+            src_ref=r.strip_send.at[d, side], dst_ref=r.strip_in.at[q, side, :, real, :],
+            send_sem=r.strip_ssem.at[j - 1, side], recv_sem=r.strip_rsem.at[j - 1, side],
             device_id={"tm": base + d}, device_id_type=mesh_ids,
         )
 
-    def edge_ref(kind, n, where):
-        if kind == 0:
-            return r.u.at[n + 1, planes, where, :]
-        if kind <= parts:
-            return r.src.at[n, pl.ds((kind - 1) * piece, piece), where, :]
-        if kind <= parts + 2:
-            return r.strip_in.at[kind - parts - 1, n, :, where, :]
-        if kind == parts + 3:
+    def strip_each(receiving, act):
+        for j in order[:3]:
+            d = q if receiving else (q + j) % group
+            for side, has in enumerate((d > 0, d < group - 1)):
+
+                @pl.when(has)
+                def _():
+                    act(strip_copy(j, side))
+
+
+    strip_kind = u_parts + parts
+    kappa_kind, kappa_strip_kind = strip_kind + 1, strip_kind + 2
+
+    def edge_ref(kind, where):
+        if kind < u_parts:
+            return r.u.at[pl.ds(1, group), pl.ds(1 + kind * u_piece, u_piece), where, :]
+        if kind < strip_kind:
+            return r.src.at[:, pl.ds((kind - u_parts) * piece, piece), where, :]
+        if kind == strip_kind:
+            return r.strip_in.at[:, :, :, where, :]
+        if kind == kappa_kind:
             return r.kap.at[:, where, :]
         return r.kap_strip.at[:, where, :]
 
-    def edge_copy(kind, n, number):
+    def edge_copy(kind, number):
         if number == 0:
             source, target = pl.ds(pad, halo), pl.ds(pad + tx, halo)
         else:
             source, target = pl.ds(pad + tx - halo, halo), pl.ds(pad - halo, halo)
         return pltpu.make_async_remote_copy(
-            src_ref=edge_ref(kind, n, source), dst_ref=edge_ref(kind, n, target),
-            send_sem=r.edge_ssem.at[kind, n, number], recv_sem=r.edge_rsem.at[kind, n, number],
+            src_ref=edge_ref(kind, source), dst_ref=edge_ref(kind, target),
+            send_sem=r.edge_ssem.at[kind, number], recv_sem=r.edge_rsem.at[kind, number],
             device_id=flanks[number][1], device_id_type=mesh_ids,
         )
 
-    def edge_start(kind, n=0):
+    def edge_start(kind):
         for number in range(2):
 
             @pl.when(flanks[number][0])
             def _():
-                edge_copy(kind, n, number).start()
-
-    def edge_send_wait(kind, n=0):
+                edge_copy(kind, number).start()
+
+    def edge_send_wait(kind):
         for number in range(2):
 
             @pl.when(flanks[number][0])
             def _():
-                edge_copy(kind, n, number).wait_send()
-
-    def edge_recv_wait(kind, n=0):
+                edge_copy(kind, number).wait_send()
+
+    def edge_recv_wait(kind):
         for number in range(2):
 
             @pl.when(flanks[number][0])
             def _():
-                edge_copy(kind, n, 1 - number).wait_recv()
+                edge_copy(kind, 1 - number).wait_recv()
 
     time_refs = [(r.u, group), (r.e1, group), (r.e2, group), (r.me1, 2), (r.me2, 2), (r.te, 1)]
     time_strips = [
@@ -205,10 +281,10 @@
                 for copy in time_copies(number):
                     copy.wait_recv()
 
-    for j in order:
-        in_copy(0, j).start()
+    for a in range(u_parts):
+        for j in order:
+            in_copy(a, j).start()
     kappa_copy.wait()
-    kappa_kind = parts + 3
     edge_start(kappa_kind)
 
     f32 = jnp.float32
@@ -226,6 +302,9 @@
                 return carry
 
             lax.fori_loop(0, nz, clear_beside, 0)
+            for n in range(group):
+                for f in range(2):
+                    r.strip_in[n, side, f, real, :] = blank(tx)
 
     lane_tx = lax.broadcasted_iota(jnp.int32, (tx, width), 1)
     lane = lax.broadcasted_iota(jnp.int32, (tx + 2 * halo, width), 1)
@@ -255,24 +334,47 @@
         packed = lax.fori_loop(0, nz, body, (nothing,) * (2 * group), unroll=2)
         for d in range(group):
             for side in range(2):
-                r.strip_send[f, d, side] = packed[2 * d + side]
+                r.strip_send[d, side, f] = packed[2 * d + side]
         for side in range(2):
-            r.strip_in[f, q, side, real, :] = r.strip_send[f, q, side]
+            r.strip_in[q, side, f, real, :] = r.strip_send[q, side, f]
 
     for f in range(2):
         own_copies[f].wait()
         pack_own(f)
-        for j in order[:3]:
-            strip_copy(f, j).start()
-        for n in range(group):
-
-            @pl.when(q == n)
-            def _():
-                edge_start(parts + 1 + f, n)
-
+    strip_each(False, lambda copy: copy.start())
     for part in range(parts):
         for j in order:
-            in_copy(1 + part, j).start()
+            in_copy(u_parts + part, j).start()
+
+    @pl.when(has_after)
+    def _():
+        before_copy().start()
+
+    @pl.when(own_work)
+    def _():
+        for copy in far_copies():
+            copy.wait()
+
+        def far_rows(p, carry):
+            for i in range(pair):
+                k = far_block - near_block + i
+                for number, row in enumerate((0, tx - 1)):
+                    r.row_send[number, 0, i, pl.ds(p, 1), :] = r.lu[1 + k, p + 1, pl.ds(halo + row, 1), :]
+                    r.row_send[number, 1, i, pl.ds(p, 1), :] = r.lkap[1 + k, p, pl.ds(row, 1), :]
+            return carry
+
+        lax.fori_loop(0, nz, far_rows, 0, unroll=4)
+        for number in range(2):
+
+            @pl.when(flanks[number][0])
+            def _():
+                row_copy(number).start()
+
+            @pl.when(jnp.logical_not(flanks[number][0]))
+            def _():
+                for f in range(2):
+                    for i in range(pair):
+                        r.row_in[number, f, i] = blank(nz)
 
     held = [(ref, 1) for ref, _ in time_refs]
     held += [(ref, 0) for ref in (r.c, r.cu, r.ce1, r.ce2, r.mc, r.cme1, r.cme2, r.tc, r.cte)]
@@ -329,7 +431,7 @@
                 r.kap_strip[side, edge, :] = blank(halo)
                 for f in range(2):
                     for n in range(group):
-                        r.strip_in[f, n, side, edge, :] = blank(halo)
+                        r.strip_in[n, side, f, edge, :] = blank(halo)
 
     for side in range(2):
 
@@ -343,8 +445,7 @@
     packed = lax.fori_loop(0, nz, kappa_body, (nothing, nothing), unroll=2)
     for side in range(2):
         r.kap_strip[side, real, :] = packed[side]
-    strip_kappa = parts + 4
-    edge_start(strip_kappa)
+    edge_start(kappa_strip_kind)
 
     level = lax.broadcasted_iota(jnp.int32, (tx + 2 * halo, width), 0)
     below = jnp.where(has_dn, damping, 0.0)
@@ -443,30 +544,24 @@
 
     wide = blank(full[1])
     edge_recv_wait(kappa_kind)
-    edge_recv_wait(strip_kappa)
+    edge_recv_wait(kappa_strip_kind)
     kappa_edge = planes_loop(lambda p, packed: pack(packed, r.kap[p, rows(full), :], p, full), wide)
 
     def arrived(a):
         in_copy(a, 0).wait()
         for j in order[:3]:
             in_copy(a, j).wait_recv()
-        for n in range(group):
-            edge_start(a, n)
-
-    arrived(0)
-    for f in range(2):
-        for j in order[:3]:
-            strip_copy(f, j).wait_recv()
-        for n in range(group):
-
-            @pl.when(q != n)
-            def _():
-                edge_start(parts + 1 + f, n)
-
+        edge_start(a)
+
+    for a in range(u_parts):
+        arrived(a)
+    strip_each(True, lambda copy: copy.wait_recv())
+    edge_start(strip_kind)
+
+    for a in range(u_parts):
+        edge_recv_wait(a)
+    edge_recv_wait(strip_kind)
     for n in range(group):
-        edge_recv_wait(0, n)
-        edge_recv_wait(parts + 1, n)
-
         def body(p, carry):
             v = r.u[n + 1, p + 1, rows(full), :]
             cc = (half * r.kap[p, rows(full), :]) * (1.0 + v * v)
@@ -477,7 +572,7 @@
         planes_loop(body, 0)
         packed = pack_planes(r.u, n + 1, full, wide)
         for side in range(2):
-            v = jnp.where(inject[side], packed, r.strip_in[0, n, side, rows(full), :])
+            v = jnp.where(inject[side], packed, r.strip_in[n, side, 0, rows(full), :])
             kk = jnp.where(inject[side], kappa_edge, r.kap_strip[side, rows(full), :])
             cc = (half * kk) * (1.0 + v * v)
             r.su[n + 1, side, rows(full), :] = v
@@ -523,8 +618,8 @@
             _, total = strip_pull(r.su, r.scu, fine, n, side, full, 1)
             r.sres[n, side, rows(full), :] = total
         if n == 1:
-            arrived(1)
-    arrived(2)
+            arrived(u_parts)
+    arrived(u_parts + 1)
 
     pairs = ((mid, fine, 2), (top, mid, 1))
     for to, of, count in pairs:
@@ -549,9 +644,6 @@
                 to.sa[n, side, rows(full), :] = diagonal
                 to.sg[n, side, rows(full), :] = r.damp[1 + side, rows(full), :] / diagonal
 
-    for n in range(group):
-        edge_recv_wait(parts + 2, n)
-
     def first_update(n, part, win):
         def body(p, carry):
             left = r.src[n, p, rows(win), :] + r.res[n, p, rows(win), :]
@@ -569,12 +661,13 @@
         for n in range(group):
             first_update(n, part, core)
         if (part + 1) * piece % out_piece == 0:
-            for j in order:
-                out_copy(0, j, (part + 1) * piece // out_piece - 1).start()
+            ready = (part + 1) * piece // out_piece - 1
+            out_each(0, ready, False, lambda copy: copy.start())
+            out_copy(0, 0, ready).start()
 
     def outer_update(part):
+        edge_recv_wait(u_parts + part)
         for n in range(group):
-            edge_recv_wait(1 + part, n)
             for win in outer:
                 first_update(n, part, win)
             packed = r.packed_one[n, rows(full), :] if part else wide
@@ -582,14 +675,14 @@
 
     for part in range(parts):
         if part > 1:
-            arrived(1 + part)
+            arrived(u_parts + part)
         inner_update(part)
         if part:
             outer_update(part - 1)
     outer_update(parts - 1)
     for n in range(group):
         for side in range(2):
-            left = r.strip_in[1, n, side, rows(full), :] + r.sres[n, side, rows(full), :]
+            left = r.strip_in[n, side, 1, rows(full), :] + r.sres[n, side, rows(full), :]
             r.sres[n, side, rows(full), :] = left
             put_values(
                 r.se1, r.sce1, fine, n, side, full, left * r.srd[n, side, rows(full), :],
@@ -679,17 +772,109 @@
         for j in order:
             out_copy(1, j, part).start()
 
-    for f in range(2):
-        for j in order[:3]:
-            strip_copy(f, j).wait_send()
-    for a in range(1 + parts):
+    @pl.when(jnp.logical_not(has_before))
+    def _():
+        def clear_before(p, carry):
+            for i in range(pair):
+                r.before[p, :, i * width : (i + 1) * width] = nothing
+            return carry
+
+        lax.fori_loop(0, nz, clear_before, 0)
+
+    @pl.when(has_before)
+    def _():
+        pltpu.make_async_remote_copy(
+            src_ref=r.before, dst_ref=r.before, send_sem=r.before_sem.at[0], recv_sem=r.before_sem.at[1],
+            device_id={"tm": me}, device_id_type=mesh_ids,
+        ).wait_recv()
+
+    far_real = pl.ds(halo, tx)
+    bare = (halo, tx)
+
+    def far_out(i):
+        return pltpu.make_async_copy(
+            r.far_res.at[i], r.res_out.at[0, 0, :, :, columns(far_block + i)], r.far_sem.at[2, i]
+        )
+
+    @pl.when(own_work)
+    def _():
+        for number in range(2):
+
+            @pl.when(flanks[number][0])
+            def _():
+                row_copy(1 - number).wait_recv()
+
+            for i in range(pair):
+                value = r.row_in[number, 0, i]
+                r.row_c[number, i] = (half * r.row_in[number, 1, i]) * (1.0 + value * value)
+        for ref in (r.lu, r.lc):
+            for k in range(pair + 3):
+                for plane in (0, nz + 1):
+                    ref[k, plane] = blank(tx + pad)
+
+            def clear_outer(p, carry):
+                for k in (0, pair + 2):
+                    ref[k, p + 1, far_real, :] = nothing
+                return carry
+
+            lax.fori_loop(0, nz, clear_outer, 0)
+
+        def far_coefficient(p, carry):
+            for k in range(pair + 1):
+                value = r.lu[1 + k, p + 1, far_real, :]
+                r.lc[1 + k, p + 1, far_real, :] = (half * r.lkap[1 + k, p]) * (1.0 + value * value)
+            for i in range(pair):
+                k = far_block - near_block + i
+                for number, row in enumerate((halo - 1, halo + tx)):
+                    r.lu[1 + k, p + 1, pl.ds(row, 1), :] = r.row_in[number, 0, i, pl.ds(p, 1), :]
+                    r.lc[1 + k, p + 1, pl.ds(row, 1), :] = r.row_c[number, i, pl.ds(p, 1), :]
+            return carry
+
+        lax.fori_loop(0, nz, far_coefficient, 0, unroll=2)
+        first_tx, last_tx = lane_tx == 0, lane_tx == width - 1
+        for i in range(pair):
+            k = 1 + far_block - near_block + i
+            own_columns = columns(far_block + i)
+
+            def body(p, carry):
+                def near_of(ref):
+                    here = ref[k, p + 1, far_real, :]
+                    before, after = ref[k - 1, p + 1, far_real, :], ref[k + 1, p + 1, far_real, :]
+                    return here, (
+                        jnp.where(first_tx, pltpu.roll(before, 1, 1), pltpu.roll(here, 1, 1)),
+                        jnp.where(last_tx, pltpu.roll(after, width - 1, 1), pltpu.roll(here, width - 1, 1)),
+                        ref[k, p + 1, pl.ds(halo - 1, tx), :], ref[k, p + 1, pl.ds(halo + 1, tx), :],
+                        ref[k, p, far_real, :], ref[k, p + 2, far_real, :],
+                    )
+
+                value, value_near = near_of(r.lu)
+                cc, c_near = near_of(r.lc)
+                left = r.own[1, p, :, own_columns] - value + r.before[p, :, i * width : (i + 1) * width]
+                for one, two in zip(value_near, c_near):
+                    left = left - (cc + two) * (value - one)
+                r.far_res[i, p] = left
+                return carry
+
+            lax.fori_loop(0, nz, body, 0, unroll=4)
+            far_out(i).start()
+        for i in range(pair):
+            far_out(i).wait()
+        for number in range(2):
+
+            @pl.when(flanks[number][0])
+            def _():
+                row_copy(number).wait_send()
+
+    @pl.when(has_after)
+    def _():
+        before_copy().wait_send()
+
+    strip_each(False, lambda copy: copy.wait_send())
+    for a in range(u_parts + parts):
         for j in order[:3]:
             in_copy(a, j).wait_send()
-    for kind in range(parts + 3):
-        for n in range(group):
-            edge_send_wait(kind, n)
-    edge_send_wait(kappa_kind)
-    edge_send_wait(strip_kappa)
+    for kind in range(u_parts + parts + 3):
+        edge_send_wait(kind)
     if chained:
 
         @pl.when(has_next)
@@ -700,12 +885,9 @@
 
     for a in range(2):
         for part in range(out_parts):
-            for j in order:
-                if j == 0:
-                    out_copy(a, j, part).wait()
-                else:
-                    out_copy(a, j, part).wait_send()
-                    out_copy(a, j, part).wait_recv()
+            out_copy(a, 0, part).wait()
+            out_each(a, part, False, lambda copy: copy.wait_send())
+            out_each(a, part, True, lambda copy: copy.wait_recv())
 
 
 def shards(tm_size, space_size, iterate, source_term, conductivity):
@@ -714,7 +896,7 @@
     tall = tx + 2 * pad
     f32 = jnp.float32
     dma = pltpu.SemaphoreType.DMA
-    kinds = parts + 5
+    kinds = u_parts + parts + 3
 
     def padded(count):
         return pltpu.VMEM((count, nz + 2, tall, width), f32)
@@ -743,17 +925,27 @@
         ("stwl", 1), ("stwr", 1), ("stwd", 1), ("stwu", 1), ("stwa", 1), ("strd", 1), ("stb", 1),
     )}
     scratch["kap_strip"] = strip()
-    scratch["strip_in"] = strip(2, group)
-    scratch["strip_send"] = pltpu.VMEM((2, group, 2, tx, width), f32)
+    scratch["strip_in"] = strip(group, 2)
+    scratch["strip_send"] = pltpu.VMEM((group, 2, 2, tx, width), f32)
     scratch["own"] = pltpu.VMEM((2, nz, tx, ty), f32)
     scratch["beside"] = pltpu.VMEM((2, nz, tx, width), f32)
+    pair = group // 2
+    scratch["lu"] = pltpu.VMEM((pair + 3, nz + 2, tx + pad, width), f32)
+    scratch["lc"] = pltpu.VMEM((pair + 3, nz + 2, tx + pad, width), f32)
+    scratch["lkap"] = pltpu.VMEM((pair + 2, nz, tx, width), f32)
+    scratch["before"] = pltpu.VMEM((nz, tx, pair * width), f32)
+    scratch["far_res"] = pltpu.VMEM((pair, nz, tx, width), f32)
+    scratch["row_send"] = pltpu.VMEM((2, 2, pair, nz, width), f32)
+    scratch["row_in"] = pltpu.VMEM((2, 2, pair, nz, width), f32)
+    scratch["row_c"] = pltpu.VMEM((2, pair, nz, width), f32)
     scratch["packed_one"] = pltpu.VMEM((group, tall, width), f32)
     scratch["damp"] = pltpu.VMEM((3, tall, width), f32)
     for name, shape in (
-        ("loc_sem", (5,)), ("in_lsem", (1 + parts,)), ("in_ssem", (1 + parts, group - 1)),
-        ("in_rsem", (1 + parts, group - 1)), ("out_lsem", (2, out_parts)), ("out_ssem", (2, out_parts, group - 1)),
-        ("out_rsem", (2, out_parts, group - 1)), ("strip_ssem", (2, group - 1)), ("strip_rsem", (2, group - 1)),
-        ("edge_ssem", (kinds, group, 2)), ("edge_rsem", (kinds, group, 2)), ("time_ssem", (6, 2)),
+        ("loc_sem", (5,)), ("in_lsem", (u_parts + parts,)), ("in_ssem", (u_parts + parts, group - 1)),
+        ("in_rsem", (u_parts + parts, group - 1)), ("out_lsem", (2, out_parts)), ("out_ssem", (2, out_parts, group - 1)),
+        ("out_rsem", (2, out_parts, group - 1)), ("strip_ssem", (group - 1, 2)), ("strip_rsem", (group - 1, 2)),
+        ("edge_ssem", (kinds, 2)), ("edge_rsem", (kinds, 2)), ("time_ssem", (6, 2)), ("far_sem", (3, pair + 1)),
+        ("before_sem", (2,)), ("row_sem", (2, 2)),
         ("time_rsem", (6, 2)),
     ):
         scratch[name] = dma(shape)

time: 61.9 us -> 61.1 us (0.987)
  Pallas kernels: 58 us -> 57.2 us
    pallas_call x1, Pallas kernels: 58 us -> 57.2 us  [shards(): pl.pallas_call(functools.partial(kernel, tm_size, space_size, names), out...]
where the time goes in v3:
time: 61.1 us; the launch traced here: 60.6 us
  Pallas kernels  57.2 us (94%)
  local copies, waits for them, and re-layouts  2.74 us (4%)
  between operations  0.65 us (1%)
    pallas_call x1, Pallas kernels, shards(): pl.pallas_call(functools.partial(kernel, tm_size, space_size, names), out...  57.2 us
    unnamed x4, local copies, waits for them, and re-layouts  2.74 us

profile of v3, /device:TPU:5, one launch (start us, length us, event | category | flops | bytes accessed | tf_op | source)
XLA Modules:
  0.0 60.6 jit_solution(5768354702656222311)
XLA Ops:
  0.6 57.2 %shard_map.50 = (f32[1,1,16,16,512]{4,3,2,1,0:T(8,128)}, f32[1,1,16,16,512]{4,3,2,1,0:T(8,128)}) custom-call(f32[1,1,16,16,512]{4,3,2,1,0:T(8,128)} %refs_0_.1, f32[1,1,16,16,512]{4,3,2,1,0:T(8,128)} %refs_1_.1, f32[1,16,16,512]{3,2,1,0:T(8,128)} %refs_2_.1), custom_call_target="tpu_custom_call" | custom-call | tf_op jit(solution)/shard_map/pallas_call | solution.py:955
  57.8 0.0 copy-start
  57.8 1.9 %copy.7 = f32[1,1,16,16,512]{4,3,2,1,0:T(8,128)} copy(f32[1,1,16,16,512]{4,3,2,1,0:T(8,128)} %get-tuple-element.4) | data formatting | bytes 1048576
  59.8 0.0 copy-done
  59.8 0.8 %copy.8 = f32[1,1,16,16,512]{4,3,2,1,0:T(8,128)} copy(f32[1,1,16,16,512]{4,3,2,1,0:T(8,128)S(1)} %copy-done) | data formatting | bytes 1048576
Async XLA Ops:
  57.8 2.0 %copy-start = (f32[1,1,16,16,512]{4,3,2,1,0:T(8,128)S(1)}, f32[1,1,16,16,512]{4,3,2,1,0:T(8,128)}, u32[]{:S(2)}) copy-start(f32[1,1,16,16,512]{4,3,2,1,0:T(8,128)} %get-tuple-element.5) | copy-start | bytes 1572868

commit v4 on v3

--- a/solution.py
+++ b/solution.py
@@ -15,7 +15,8 @@
 pad = 2 * halo
 u_parts = 2
 parts = 4
-out_parts = 2
+passes = (2, 3, 4)
+stages = 5
 mesh_ids = pl.DeviceIdType.MESH
 order = (2, 1, 3, 0)
 unroll = 8
@@ -28,7 +29,16 @@
     span = width // nz
     chained = tm_size > group
     half = 0.5 * tau_step
-    piece, u_piece, out_piece = nz // parts, nz // u_parts, nz // out_parts
+    piece, u_piece = nz // parts, nz // u_parts
+
+    def reach(number, stage):
+        bounds = [0] + [known * piece - stage if known < parts else nz for known in passes]
+        return max(bounds[number], 0), bounds[number + 1]
+
+    pieces = [[(0, nz // 2), (nz // 2, nz // 2)], []]
+    for number in range(len(passes)):
+        first, last = reach(number, stages)
+        pieces[1].append((first, last - first))
 
     full = (pad - halo, tx + 2 * halo)
     trim = (pad - halo // 2, tx + halo)
@@ -159,7 +169,7 @@
 
     def out_copy(a, j, part):
         d = (q + j) % group
-        some = pl.ds(part * out_piece, out_piece)
+        some = pl.ds(*pieces[a][part])
         hbm = (r.res_out, r.new_out)[a].at[0, 0, some, :, columns(q)]
         held = (r.res, r.new)[a].at[d, some, real, :]
         if j == 0:
@@ -660,10 +670,10 @@
     def inner_update(part):
         for n in range(group):
             first_update(n, part, core)
-        if (part + 1) * piece % out_piece == 0:
-            ready = (part + 1) * piece // out_piece - 1
-            out_each(0, ready, False, lambda copy: copy.start())
-            out_copy(0, 0, ready).start()
+        for number, (first, count) in enumerate(pieces[0]):
+            if first + count == (part + 1) * piece:
+                out_each(0, number, False, lambda copy: copy.start())
+                out_copy(0, 0, number).start()
 
     def outer_update(part):
         edge_recv_wait(u_parts + part)
@@ -673,27 +683,18 @@
             packed = r.packed_one[n, rows(full), :] if part else wide
             r.packed_one[n, rows(full), :] = pack_planes(r.e1, n + 1, full, packed, part * piece, piece)
 
-    for part in range(parts):
-        if part > 1:
-            arrived(u_parts + part)
-        inner_update(part)
-        if part:
-            outer_update(part - 1)
-    outer_update(parts - 1)
-    for n in range(group):
-        for side in range(2):
-            left = r.strip_in[n, side, 1, rows(full), :] + r.sres[n, side, rows(full), :]
-            r.sres[n, side, rows(full), :] = left
-            put_values(
-                r.se1, r.sce1, fine, n, side, full, left * r.srd[n, side, rows(full), :],
-                r.packed_one[n, rows(full), :], 1,
-            )
-    time_send(1)
-    time_wait(1)
-
     narrow = blank(trim[1])
 
-    def again(w, v, cv, sv, scv, b, sb, to_v, to_cv, to_sv, to_scv, count):
+    def pack_more(stage, ref, n, number):
+        first, last = reach(number, stage)
+        packed = r.packs[stage - 1, n, rows(trim), :] if number else narrow
+        packed = pack_planes(ref, n + 1, trim, packed, first, last - first)
+        if number < len(passes) - 1:
+            r.packs[stage - 1, n, rows(trim), :] = packed
+        return packed
+
+    def again(number, stage, w, v, cv, sv, scv, b, sb, to_v, to_cv, to_sv, to_scv, count):
+        first, last = reach(number, stage)
         for n in range(count):
             ghost = ghosts(sv, n + 1, trim)
 
@@ -705,22 +706,23 @@
                 to_cv[n, p + 1, rows(trim), :] = w.c[n, p + 1, rows(trim), :] * update
                 return carry
 
-            planes_loop(body, 0)
-            packed = pack_planes(to_v, n + 1, trim, narrow)
+            planes_loop(body, 0, first, last - first)
+            packed = pack_more(stage, to_v, n, number)
             for side in range(2):
                 value, total = strip_pull(sv, scv, w, n, side, trim, 1)
                 left = sb[n, side, rows(trim), :] + total
                 update = value + left * w.sg[n, side, rows(trim), :]
                 put_values(to_sv, to_scv, w, n, side, trim, update, packed, 1)
 
-    def coarsen(w, to, v, cv, sv, scv, b, sb, to_b, to_sb, to_v, to_cv, to_sv, to_scv, count):
+    def coarsen(number, stage, w, to, v, cv, sv, scv, b, sb, to_b, to_sb, to_v, to_cv, to_sv, to_scv, count):
+        first, last = reach(number, stage)
         for n in range(count):
-            pair = [ghosts(sv, 2 * n + i + 1, trim) for i in range(2)]
+            both = [ghosts(sv, 2 * n + i + 1, trim) for i in range(2)]
 
             def body(p, carry):
                 rhs = None
                 for i in range(2):
-                    _, total = pull(v, cv, w, 2 * n + i, pair[i], p, trim, 1)
+                    _, total = pull(v, cv, w, 2 * n + i, both[i], p, trim, 1)
                     left = b[2 * n + i, p, rows(trim), :] + total
                     rhs = left if rhs is None else rhs + left
                 to_b[n, p, rows(trim), :] = rhs
@@ -729,8 +731,8 @@
                 to_cv[n, p + 1, rows(trim), :] = to.c[n, p + 1, rows(trim), :] * update
                 return carry
 
-            planes_loop(body, 0)
-            packed = pack_planes(to_v, n + 1, trim, narrow)
+            planes_loop(body, 0, first, last - first)
+            packed = pack_more(stage, to_v, n, number)
             for side in range(2):
                 rhs = None
                 for i in range(2):
@@ -741,36 +743,66 @@
                 update = rhs * to.sg[n, side, rows(trim), :]
                 put_values(to_sv, to_scv, to, n, side, trim, update, packed, 1)
 
-    again(fine, r.e1, r.ce1, r.se1, r.sce1, r.res, r.sres, r.e2, r.ce2, r.se2, r.sce2, group)
-    time_send(2)
-    time_wait(2)
-    coarsen(
-        fine, mid, r.e2, r.ce2, r.se2, r.sce2, r.res, r.sres, r.mb, r.smb, r.me1, r.cme1, r.sme1, r.scme1, 2
-    )
-    time_send(3)
-    time_wait(3)
-    again(mid, r.me1, r.cme1, r.sme1, r.scme1, r.mb, r.smb, r.me2, r.cme2, r.sme2, r.scme2, 2)
-    time_send(4)
-    time_wait(4)
-    coarsen(
-        mid, top, r.me2, r.cme2, r.sme2, r.scme2, r.mb, r.smb, r.tb, r.stb, r.te, r.cte, r.ste, r.scte, 1
-    )
-    time_send(5)
-    time_wait(5)
-    ghost = ghosts(r.ste, 1, core)
-
-    def body(p, carry):
-        value, total = pull(r.te, r.cte, top, 0, ghost, p, core, 1)
-        update = value + (r.tb[0, p, real, :] + total) * r.trd[0, p, real, :]
+    def run_pass(number):
+        started, ended = number == 0, number == len(passes) - 1
+
+        def meet(level):
+            if ended:
+                time_send(level)
+            if started:
+                time_wait(level)
+
         for n in range(group):
-            middle = r.me2[n // 2 + 1, p + 1, real, :] + update
-            r.new[n, p, real, :] = r.u[n + 1, p + 1, real, :] + (r.e2[n + 1, p + 1, real, :] + middle)
-        return carry
-
-    for part in range(out_parts):
-        planes_loop(body, 0, part * out_piece, out_piece)
-        for j in order:
-            out_copy(1, j, part).start()
+            for side in range(2):
+                put_values(
+                    r.se1, r.sce1, fine, n, side, full, r.sres[n, side, rows(full), :] * r.srd[n, side, rows(full), :],
+                    r.packed_one[n, rows(full), :], 1,
+                )
+        meet(1)
+        again(number, 1, fine, r.e1, r.ce1, r.se1, r.sce1, r.res, r.sres, r.e2, r.ce2, r.se2, r.sce2, group)
+        meet(2)
+        coarsen(
+            number, 2, fine, mid, r.e2, r.ce2, r.se2, r.sce2, r.res, r.sres, r.mb, r.smb, r.me1, r.cme1, r.sme1,
+            r.scme1, 2,
+        )
+        meet(3)
+        again(number, 3, mid, r.me1, r.cme1, r.sme1, r.scme1, r.mb, r.smb, r.me2, r.cme2, r.sme2, r.scme2, 2)
+        meet(4)
+        coarsen(
+            number, 4, mid, top, r.me2, r.cme2, r.sme2, r.scme2, r.mb, r.smb, r.tb, r.stb, r.te, r.cte, r.ste, r.scte,
+            1,
+        )
+        meet(5)
+        ghost = ghosts(r.ste, 1, core)
+
+        def body(p, carry):
+            value, total = pull(r.te, r.cte, top, 0, ghost, p, core, 1)
+            update = value + (r.tb[0, p, real, :] + total) * r.trd[0, p, real, :]
+            for n in range(group):
+                middle = r.me2[n // 2 + 1, p + 1, real, :] + update
+                r.new[n, p, real, :] = r.u[n + 1, p + 1, real, :] + (r.e2[n + 1, p + 1, real, :] + middle)
+            return carry
+
+        first, last = reach(number, stages)
+        planes_loop(body, 0, first, last - first)
+        out_each(1, number, False, lambda copy: copy.start())
+        out_copy(1, 0, number).start()
+
+    for n in range(group):
+        for side in range(2):
+            r.sres[n, side, rows(full), :] = (
+                r.strip_in[n, side, 1, rows(full), :] + r.sres[n, side, rows(full), :]
+            )
+    for part in range(parts):
+        if part > 1:
+            arrived(u_parts + part)
+        inner_update(part)
+        if part:
+            outer_update(part - 1)
+            if part in passes:
+                run_pass(passes.index(part))
+    outer_update(parts - 1)
+    run_pass(len(passes) - 1)
 
     @pl.when(jnp.logical_not(has_before))
     def _():
@@ -884,7 +916,7 @@
                     copy.wait_send()
 
     for a in range(2):
-        for part in range(out_parts):
+        for part in range(len(pieces[a])):
             out_copy(a, 0, part).wait()
             out_each(a, part, False, lambda copy: copy.wait_send())
             out_each(a, part, True, lambda copy: copy.wait_recv())
@@ -938,12 +970,13 @@
     scratch["row_send"] = pltpu.VMEM((2, 2, pair, nz, width), f32)
     scratch["row_in"] = pltpu.VMEM((2, 2, pair, nz, width), f32)
     scratch["row_c"] = pltpu.VMEM((2, pair, nz, width), f32)
+    scratch["packs"] = pltpu.VMEM((stages - 1, group, tall, width), f32)
     scratch["packed_one"] = pltpu.VMEM((group, tall, width), f32)
     scratch["damp"] = pltpu.VMEM((3, tall, width), f32)
     for name, shape in (
         ("loc_sem", (5,)), ("in_lsem", (u_parts + parts,)), ("in_ssem", (u_parts + parts, group - 1)),
-        ("in_rsem", (u_parts + parts, group - 1)), ("out_lsem", (2, out_parts)), ("out_ssem", (2, out_parts, group - 1)),
-        ("out_rsem", (2, out_parts, group - 1)), ("strip_ssem", (group - 1, 2)), ("strip_rsem", (group - 1, 2)),
+        ("in_rsem", (u_parts + parts, group - 1)), ("out_lsem", (2, len(passes) + 1)), ("out_ssem", (2, len(passes) + 1, group - 1)),
+        ("out_rsem", (2, len(passes) + 1, group - 1)), ("strip_ssem", (group - 1, 2)), ("strip_rsem", (group - 1, 2)),
         ("edge_ssem", (kinds, 2)), ("edge_rsem", (kinds, 2)), ("time_ssem", (6, 2)), ("far_sem", (3, pair + 1)),
         ("before_sem", (2,)), ("row_sem", (2, 2)),
         ("time_rsem", (6, 2)),

time: 61.1 us -> 55.6 us (0.910)
  Pallas kernels: 57.2 us -> 51.3 us
    pallas_call x1, Pallas kernels: 57.2 us -> 51.3 us  [shards(): pl.pallas_call(functools.partial(kernel, tm_size, space_size, names), out...]
where the time goes in v4:
time: 55.6 us; the launch traced here: 54.7 us
  Pallas kernels  51.3 us (92%)
  local copies, waits for them, and re-layouts  2.74 us (5%)
  between operations  0.65 us (1%)
    pallas_call x1, Pallas kernels, shards(): pl.pallas_call(functools.partial(kernel, tm_size, space_size, names), out...  51.3 us
    unnamed x4, local copies, waits for them, and re-layouts  2.74 us

profile of v4, /device:TPU:5, one launch (start us, length us, event | category | flops | bytes accessed | tf_op | source)
XLA Modules:
  0.0 54.7 jit_solution(10009359914131515462)
XLA Ops:
  0.6 51.3 %shard_map.50 = (f32[1,1,16,16,512]{4,3,2,1,0:T(8,128)}, f32[1,1,16,16,512]{4,3,2,1,0:T(8,128)}) custom-call(f32[1,1,16,16,512]{4,3,2,1,0:T(8,128)} %refs_0_.1, f32[1,1,16,16,512]{4,3,2,1,0:T(8,128)} %refs_1_.1, f32[1,16,16,512]{3,2,1,0:T(8,128)} %refs_2_.1), custom_call_target="tpu_custom_call" | custom-call | tf_op jit(solution)/shard_map/pallas_call | solution.py:988
  52.0 0.0 copy-start
  52.0 1.9 %copy.7 = f32[1,1,16,16,512]{4,3,2,1,0:T(8,128)} copy(f32[1,1,16,16,512]{4,3,2,1,0:T(8,128)} %get-tuple-element.4) | data formatting | bytes 1048576
  53.9 0.0 copy-done
  53.9 0.8 %copy.8 = f32[1,1,16,16,512]{4,3,2,1,0:T(8,128)} copy(f32[1,1,16,16,512]{4,3,2,1,0:T(8,128)S(1)} %copy-done) | data formatting | bytes 1048576
Async XLA Ops:
  52.0 2.0 %copy-start = (f32[1,1,16,16,512]{4,3,2,1,0:T(8,128)S(1)}, f32[1,1,16,16,512]{4,3,2,1,0:T(8,128)}, u32[]{:S(2)}) copy-start(f32[1,1,16,16,512]{4,3,2,1,0:T(8,128)} %get-tuple-element.5) | copy-start | bytes 1572868

commit v5 on v4

--- a/solution.py
+++ b/solution.py
@@ -14,8 +14,9 @@
 halo = 8
 pad = 2 * halo
 u_parts = 2
-parts = 4
-passes = (2, 3, 4)
+shares = (6, 6, 4)
+parts = len(shares)
+passes = (1, 2, 3)
 stages = 5
 mesh_ids = pl.DeviceIdType.MESH
 order = (2, 1, 3, 0)
@@ -29,13 +30,15 @@
     span = width // nz
     chained = tm_size > group
     half = 0.5 * tau_step
-    piece, u_piece = nz // parts, nz // u_parts
+    u_piece = nz // u_parts
+    cuts = [nz * sum(shares[:k]) // sum(shares) for k in range(parts + 1)]
+    spans = [(cuts[k], cuts[k + 1] - cuts[k]) for k in range(parts)]
 
     def reach(number, stage):
-        bounds = [0] + [known * piece - stage if known < parts else nz for known in passes]
+        bounds = [0] + [cuts[known] - stage if known < parts else nz for known in passes]
         return max(bounds[number], 0), bounds[number + 1]
 
-    pieces = [[(0, nz // 2), (nz // 2, nz // 2)], []]
+    pieces = [[(0, cuts[-2]), spans[-1]], []]
     for number in range(len(passes)):
         first, last = reach(number, stages)
         pieces[1].append((first, last - first))
@@ -158,7 +161,7 @@
             hbm = r.state_in.at[0, 0, some, :, columns(d)]
             dst = r.u.at[q + 1, pl.ds(1 + a * u_piece, u_piece), real, :]
         else:
-            some = pl.ds((a - u_parts) * piece, piece)
+            some = pl.ds(*spans[a - u_parts])
             hbm, dst = r.source_in.at[0, 0, some, :, columns(d)], r.src.at[q, some, real, :]
         if j == 0:
             return pltpu.make_async_copy(hbm, dst, r.in_lsem.at[a])
@@ -217,7 +220,7 @@
         if kind < u_parts:
             return r.u.at[pl.ds(1, group), pl.ds(1 + kind * u_piece, u_piece), where, :]
         if kind < strip_kind:
-            return r.src.at[:, pl.ds((kind - u_parts) * piece, piece), where, :]
+            return r.src.at[:, pl.ds(*spans[kind - u_parts]), where, :]
         if kind == strip_kind:
             return r.strip_in.at[:, :, :, where, :]
         if kind == kappa_kind:
@@ -291,9 +294,8 @@
                 for copy in time_copies(number):
                     copy.wait_recv()
 
-    for a in range(u_parts):
-        for j in order:
-            in_copy(a, j).start()
+    for j in order:
+        in_copy(0, j).start()
     kappa_copy.wait()
     edge_start(kappa_kind)
 
@@ -352,9 +354,9 @@
         own_copies[f].wait()
         pack_own(f)
     strip_each(False, lambda copy: copy.start())
-    for part in range(parts):
+    for a in range(1, u_parts + parts):
         for j in order:
-            in_copy(u_parts + part, j).start()
+            in_copy(a, j).start()
 
     @pl.when(has_after)
     def _():
@@ -478,11 +480,11 @@
     def pack(packed, value, p, win):
         return jnp.where(cut(plane_lane, win) == p, pltpu.roll(value, span * p + 2, 1), packed)
 
-    def pack_planes(ref, n, win, packed, first=0, count=None):
+    def pack_planes(ref, count, win, packed, first=0, planes_count=None):
         def body(p, packed):
-            return pack(packed, ref[n, p + 1, rows(win), :], p, win)
-
-        return planes_loop(body, packed, first, count)
+            return tuple(pack(packed[n], ref[n + 1, p + 1, rows(win), :], p, win) for n in range(count))
+
+        return planes_loop(body, tuple(packed), first, planes_count)
 
     def ghosts(ref, n, win):
         left = pltpu.roll(ref[n, 0, rows(win), :], 1, 1)
@@ -563,34 +565,79 @@
             in_copy(a, j).wait_recv()
         edge_start(a)
 
-    for a in range(u_parts):
-        arrived(a)
+    def coefficients(p, carry):
+        scaled = half * r.kap[p, rows(full), :]
+        for n in range(group):
+            v = r.u[n + 1, p + 1, rows(full), :]
+            cc = scaled * (1.0 + v * v)
+            r.c[n, p + 1, rows(full), :] = cc
+            r.cu[n, p + 1, rows(full), :] = cc * v
+        return carry
+
+    def strip_coefficients(packed):
+        for n in range(group):
+            for side in range(2):
+                v = jnp.where(inject[side], packed[n], r.strip_in[n, side, 0, rows(full), :])
+                kk = jnp.where(inject[side], kappa_edge, r.kap_strip[side, rows(full), :])
+                cc = (half * kk) * (1.0 + v * v)
+                r.su[n + 1, side, rows(full), :] = v
+                r.sc[n, side, rows(full), :] = cc
+                r.scu[n, side, rows(full), :] = cc * v
+
+    def weights(first, count):
+        for n in range(group):
+            ghost_c, ghost_u = ghosts(r.sc, n, full), ghosts(r.su, n + 1, full)
+
+            def body(p, carry):
+                cc = r.c[n, p + 1, rows(full), :]
+                left, right = sideways(cc, ghost_c, p, full)
+                left, right = cc + left, cc + right
+                r.wl[n, p, rows(full), :] = left
+                r.wr[n, p, rows(full), :] = right
+                diagonal = 1.0 + ((4.0 * cc + left) + (right + across(r.c, n, p, full)))
+                r.wa[n, p, rows(full), :] = diagonal
+                r.rd[n, p, rows(full), :] = r.damp[0, rows(full), :] / diagonal
+                _, total = pull(r.u, r.cu, fine, n, ghost_u, p, full, 1)
+                r.res[n, p, rows(full), :] = total
+                return carry
+
+            planes_loop(body, 0, first, count)
+
+    def coarser(first, count):
+        for to, of, slices in ((mid, fine, 2), (top, mid, 1)):
+
+            def body(p, carry):
+                for n in range(slices):
+                    to.c[n, p + 1, rows(full), :] = of.c[2 * n, p + 1, rows(full), :] + of.c[2 * n + 1, p + 1, rows(full), :]
+                    for one, two in ((to.l, of.l), (to.r, of.r)):
+                        one[n, p, rows(full), :] = two[2 * n, p, rows(full), :] + two[2 * n + 1, p, rows(full), :]
+                    diagonal = (of.a[2 * n, p, rows(full), :] - 1.0) + of.a[2 * n + 1, p, rows(full), :]
+                    to.a[n, p, rows(full), :] = diagonal
+                    to.d[n, p, rows(full), :] = r.damp[0, rows(full), :] / diagonal
+                return carry
+
+            lax.fori_loop(first, first + count, body, 0, unroll=min(4, count))
+
+    arrived(0)
     strip_each(True, lambda copy: copy.wait_recv())
     edge_start(strip_kind)
-
-    for a in range(u_parts):
+    edge_recv_wait(0)
+    edge_recv_wait(strip_kind)
+    strip_coefficients((wide,) * group)
+    lax.fori_loop(0, u_piece, coefficients, 0, unroll=4)
+    time_wait(0)
+    known = u_piece - 1
+    weights(0, known)
+    for a in range(1, u_parts):
+        arrived(a)
+    coarser(0, known)
+    packed_u = pack_planes(r.u, group, full, (wide,) * group, 0, u_piece)
+    for a in range(1, u_parts):
         edge_recv_wait(a)
-    edge_recv_wait(strip_kind)
-    for n in range(group):
-        def body(p, carry):
-            v = r.u[n + 1, p + 1, rows(full), :]
-            cc = (half * r.kap[p, rows(full), :]) * (1.0 + v * v)
-            r.c[n, p + 1, rows(full), :] = cc
-            r.cu[n, p + 1, rows(full), :] = cc * v
-            return carry
-
-        planes_loop(body, 0)
-        packed = pack_planes(r.u, n + 1, full, wide)
-        for side in range(2):
-            v = jnp.where(inject[side], packed, r.strip_in[n, side, 0, rows(full), :])
-            kk = jnp.where(inject[side], kappa_edge, r.kap_strip[side, rows(full), :])
-            cc = (half * kk) * (1.0 + v * v)
-            r.su[n + 1, side, rows(full), :] = v
-            r.sc[n, side, rows(full), :] = cc
-            r.scu[n, side, rows(full), :] = cc * v
+    lax.fori_loop(u_piece, nz, coefficients, 0, unroll=4)
+    packed_u = pack_planes(r.u, group, full, packed_u, u_piece, nz - u_piece)
+    strip_coefficients(packed_u)
     time_send(0)
-    time_wait(0)
-
     for n in range(group):
         for side in range(2):
             cc = r.sc[n, side, rows(full), :]
@@ -599,52 +646,23 @@
                 (r.swl, 1, None), (r.swr, width - 1, None),
                 (r.swd, span, first_plane[side]), (r.swu, width - span, last_plane[side]),
             ):
-                near = pltpu.roll(cc, shift, 1)
-                weight = cc + near
+                beside = pltpu.roll(cc, shift, 1)
+                weight = cc + beside
                 if off is not None:
-                    near, weight = jnp.where(off, 0.0, near), jnp.where(off, 0.0, weight)
+                    beside, weight = jnp.where(off, 0.0, beside), jnp.where(off, 0.0, weight)
                 ref[n, side, rows(full), :] = weight
-                total = total + near
+                total = total + beside
             diagonal = 1.0 + (6.0 * cc + total)
             r.swa[n, side, rows(full), :] = diagonal
             r.srd[n, side, rows(full), :] = r.damp[1 + side, rows(full), :] / diagonal
-        ghost_c, ghost_u = ghosts(r.sc, n, full), ghosts(r.su, n + 1, full)
-
-        def body(p, carry):
-            cc = r.c[n, p + 1, rows(full), :]
-            left, right = sideways(cc, ghost_c, p, full)
-            left, right = cc + left, cc + right
-            r.wl[n, p, rows(full), :] = left
-            r.wr[n, p, rows(full), :] = right
-            diagonal = 1.0 + ((4.0 * cc + left) + (right + across(r.c, n, p, full)))
-            r.wa[n, p, rows(full), :] = diagonal
-            r.rd[n, p, rows(full), :] = r.damp[0, rows(full), :] / diagonal
-            _, total = pull(r.u, r.cu, fine, n, ghost_u, p, full, 1)
-            r.res[n, p, rows(full), :] = total
-            return carry
-
-        planes_loop(body, 0)
+    weights(known, nz - known)
+    arrived(u_parts)
+    for n in range(group):
         for side in range(2):
             _, total = strip_pull(r.su, r.scu, fine, n, side, full, 1)
             r.sres[n, side, rows(full), :] = total
-        if n == 1:
-            arrived(u_parts)
-    arrived(u_parts + 1)
-
-    pairs = ((mid, fine, 2), (top, mid, 1))
-    for to, of, count in pairs:
-        for n in range(count):
-
-            def body(p, carry):
-                to.c[n, p + 1, rows(full), :] = of.c[2 * n, p + 1, rows(full), :] + of.c[2 * n + 1, p + 1, rows(full), :]
-                for one, two in ((to.l, of.l), (to.r, of.r)):
-                    one[n, p, rows(full), :] = two[2 * n, p, rows(full), :] + two[2 * n + 1, p, rows(full), :]
-                diagonal = (of.a[2 * n, p, rows(full), :] - 1.0) + of.a[2 * n + 1, p, rows(full), :]
-                to.a[n, p, rows(full), :] = diagonal
-                to.d[n, p, rows(full), :] = r.damp[0, rows(full), :] / diagonal
-                return carry
-
-            planes_loop(body, 0)
+    for to, of, slices in ((mid, fine, 2), (top, mid, 1)):
+        for n in range(slices):
             for side in range(2):
                 for one, two in (
                     (to.sc, of.sc), (to.sl, of.sl), (to.sr, of.sr), (to.sd, of.sd), (to.su, of.su),
@@ -653,95 +671,98 @@
                 diagonal = (of.sa[2 * n, side, rows(full), :] - 1.0) + of.sa[2 * n + 1, side, rows(full), :]
                 to.sa[n, side, rows(full), :] = diagonal
                 to.sg[n, side, rows(full), :] = r.damp[1 + side, rows(full), :] / diagonal
-
-    def first_update(n, part, win):
+    coarser(known, nz - known)
+
+    def first_update(part, wins):
         def body(p, carry):
-            left = r.src[n, p, rows(win), :] + r.res[n, p, rows(win), :]
-            r.res[n, p, rows(win), :] = left
-            update = left * r.rd[n, p, rows(win), :]
-            r.e1[n + 1, p + 1, rows(win), :] = update
-            r.ce1[n, p + 1, rows(win), :] = r.c[n, p + 1, rows(win), :] * update
+            for n in range(group):
+                for win in wins:
+                    left = r.src[n, p, rows(win), :] + r.res[n, p, rows(win), :]
+                    r.res[n, p, rows(win), :] = left
+                    update = left * r.rd[n, p, rows(win), :]
+                    r.e1[n + 1, p + 1, rows(win), :] = update
+                    r.ce1[n, p + 1, rows(win), :] = r.c[n, p + 1, rows(win), :] * update
             return carry
 
-        planes_loop(body, 0, part * piece, piece)
-
-    outer = [(pad - halo, halo), (pad + tx, halo)]
+        planes_loop(body, 0, *spans[part])
 
     def inner_update(part):
-        for n in range(group):
-            first_update(n, part, core)
+        first_update(part, [core])
         for number, (first, count) in enumerate(pieces[0]):
-            if first + count == (part + 1) * piece:
+            if first + count == cuts[part + 1]:
                 out_each(0, number, False, lambda copy: copy.start())
                 out_copy(0, 0, number).start()
 
     def outer_update(part):
         edge_recv_wait(u_parts + part)
+        first_update(part, [(pad - halo, halo), (pad + tx, halo)])
+        packed = [r.packed_one[n, rows(full), :] if part else wide for n in range(group)]
+        packed = pack_planes(r.e1, group, full, packed, *spans[part])
         for n in range(group):
-            for win in outer:
-                first_update(n, part, win)
-            packed = r.packed_one[n, rows(full), :] if part else wide
-            r.packed_one[n, rows(full), :] = pack_planes(r.e1, n + 1, full, packed, part * piece, piece)
+            r.packed_one[n, rows(full), :] = packed[n]
 
     narrow = blank(trim[1])
 
-    def pack_more(stage, ref, n, number):
+    def pack_more(stage, ref, count, number):
         first, last = reach(number, stage)
-        packed = r.packs[stage - 1, n, rows(trim), :] if number else narrow
-        packed = pack_planes(ref, n + 1, trim, packed, first, last - first)
+        packed = [r.packs[stage - 1, n, rows(trim), :] if number else narrow for n in range(count)]
+        packed = pack_planes(ref, count, trim, packed, first, last - first)
         if number < len(passes) - 1:
-            r.packs[stage - 1, n, rows(trim), :] = packed
+            for n in range(count):
+                r.packs[stage - 1, n, rows(trim), :] = packed[n]
         return packed
 
     def again(number, stage, w, v, cv, sv, scv, b, sb, to_v, to_cv, to_sv, to_scv, count):
         first, last = reach(number, stage)
-        for n in range(count):
-            ghost = ghosts(sv, n + 1, trim)
-
-            def body(p, carry):
-                value, total = pull(v, cv, w, n, ghost, p, trim, 1)
+        ghost = [ghosts(sv, n + 1, trim) for n in range(count)]
+
+        def body(p, carry):
+            for n in range(count):
+                value, total = pull(v, cv, w, n, ghost[n], p, trim, 1)
                 left = b[n, p, rows(trim), :] + total
                 update = value + left * w.d[n, p, rows(trim), :]
                 to_v[n + 1, p + 1, rows(trim), :] = update
                 to_cv[n, p + 1, rows(trim), :] = w.c[n, p + 1, rows(trim), :] * update
-                return carry
-
-            planes_loop(body, 0, first, last - first)
-            packed = pack_more(stage, to_v, n, number)
+            return carry
+
+        planes_loop(body, 0, first, last - first)
+        packed = pack_more(stage, to_v, count, number)
+        for n in range(count):
             for side in range(2):
                 value, total = strip_pull(sv, scv, w, n, side, trim, 1)
                 left = sb[n, side, rows(trim), :] + total
                 update = value + left * w.sg[n, side, rows(trim), :]
-                put_values(to_sv, to_scv, w, n, side, trim, update, packed, 1)
+                put_values(to_sv, to_scv, w, n, side, trim, update, packed[n], 1)
 
     def coarsen(number, stage, w, to, v, cv, sv, scv, b, sb, to_b, to_sb, to_v, to_cv, to_sv, to_scv, count):
         first, last = reach(number, stage)
-        for n in range(count):
-            both = [ghosts(sv, 2 * n + i + 1, trim) for i in range(2)]
-
-            def body(p, carry):
+        ghost = [ghosts(sv, n + 1, trim) for n in range(2 * count)]
+
+        def body(p, carry):
+            for n in range(count):
                 rhs = None
-                for i in range(2):
-                    _, total = pull(v, cv, w, 2 * n + i, both[i], p, trim, 1)
-                    left = b[2 * n + i, p, rows(trim), :] + total
+                for m in (2 * n, 2 * n + 1):
+                    _, total = pull(v, cv, w, m, ghost[m], p, trim, 1)
+                    left = b[m, p, rows(trim), :] + total
                     rhs = left if rhs is None else rhs + left
                 to_b[n, p, rows(trim), :] = rhs
                 update = rhs * to.d[n, p, rows(trim), :]
                 to_v[n + 1, p + 1, rows(trim), :] = update
                 to_cv[n, p + 1, rows(trim), :] = to.c[n, p + 1, rows(trim), :] * update
-                return carry
-
-            planes_loop(body, 0, first, last - first)
-            packed = pack_more(stage, to_v, n, number)
+            return carry
+
+        planes_loop(body, 0, first, last - first)
+        packed = pack_more(stage, to_v, count, number)
+        for n in range(count):
             for side in range(2):
                 rhs = None
-                for i in range(2):
-                    _, total = strip_pull(sv, scv, w, 2 * n + i, side, trim, 1)
-                    left = sb[2 * n + i, side, rows(trim), :] + total
+                for m in (2 * n, 2 * n + 1):
+                    _, total = strip_pull(sv, scv, w, m, side, trim, 1)
+                    left = sb[m, side, rows(trim), :] + total
                     rhs = left if rhs is None else rhs + left
                 to_sb[n, side, rows(trim), :] = rhs
                 update = rhs * to.sg[n, side, rows(trim), :]
-                put_values(to_sv, to_scv, to, n, side, trim, update, packed, 1)
+                put_values(to_sv, to_scv, to, n, side, trim, update, packed[n], 1)
 
     def run_pass(number):
         started, ended = number == 0, number == len(passes) - 1
@@ -794,7 +815,7 @@
                 r.strip_in[n, side, 1, rows(full), :] + r.sres[n, side, rows(full), :]
             )
     for part in range(parts):
-        if part > 1:
+        if part:
             arrived(u_parts + part)
         inner_update(part)
         if part:

time: 55.6 us -> 52.7 us (0.948)
  Pallas kernels: 51.3 us -> 49 us
    pallas_call x1, Pallas kernels: 51.3 us -> 49 us  [shards(): pl.pallas_call(functools.partial(kernel, tm_size, space_size, names), out...]
where the time goes in v5:
time: 52.7 us; the launch traced here: 52.3 us
  Pallas kernels  49 us (93%)
  local copies, waits for them, and re-layouts  2.74 us (5%)
  between operations  0.65 us (1%)
    pallas_call x1, Pallas kernels, shards(): pl.pallas_call(functools.partial(kernel, tm_size, space_size, names), out...  49 us
    unnamed x4, local copies, waits for them, and re-layouts  2.74 us

profile of v5, /device:TPU:5, one launch (start us, length us, event | category | flops | bytes accessed | tf_op | source)
XLA Modules:
  0.0 52.3 jit_solution(1391889833342913286)
XLA Ops:
  0.6 49.0 %shard_map.50 = (f32[1,1,16,16,512]{4,3,2,1,0:T(8,128)}, f32[1,1,16,16,512]{4,3,2,1,0:T(8,128)}) custom-call(f32[1,1,16,16,512]{4,3,2,1,0:T(8,128)} %refs_0_.1, f32[1,1,16,16,512]{4,3,2,1,0:T(8,128)} %refs_1_.1, f32[1,16,16,512]{3,2,1,0:T(8,128)} %refs_2_.1), custom_call_target="tpu_custom_call" | custom-call | tf_op jit(solution)/shard_map/pallas_call | solution.py:1009
  49.6 0.0 copy-start
  49.6 1.9 %copy.7 = f32[1,1,16,16,512]{4,3,2,1,0:T(8,128)} copy(f32[1,1,16,16,512]{4,3,2,1,0:T(8,128)} %get-tuple-element.4) | data formatting | bytes 1048576
  51.5 0.0 copy-done
  51.5 0.8 %copy.8 = f32[1,1,16,16,512]{4,3,2,1,0:T(8,128)} copy(f32[1,1,16,16,512]{4,3,2,1,0:T(8,128)S(1)} %copy-done) | data formatting | bytes 1048576
Async XLA Ops:
  49.6 2.0 %copy-start = (f32[1,1,16,16,512]{4,3,2,1,0:T(8,128)S(1)}, f32[1,1,16,16,512]{4,3,2,1,0:T(8,128)}, u32[]{:S(2)}) copy-start(f32[1,1,16,16,512]{4,3,2,1,0:T(8,128)} %get-tuple-element.5) | copy-start | bytes 1572868

commit v6 on v5

--- a/solution.py
+++ b/solution.py
@@ -1006,16 +1006,41 @@
     names = ("state_in", "source_in", "kappa_in", "new_out", "res_out", *scratch)
     out = jax.ShapeDtypeStruct(iterate.shape, f32)
     hbm = pl.BlockSpec(memory_space=pltpu.HBM)
-    return pl.pallas_call(
+    new, res = pl.pallas_call(
         functools.partial(kernel, tm_size, space_size, names),
-        out_shape=(out, out),
+        out_shape=(pltpu.VMEM(iterate.shape, f32),) * 2,
         in_specs=[hbm] * 3,
-        out_specs=(hbm, hbm),
+        out_specs=(pl.BlockSpec(memory_space=pltpu.VMEM),) * 2,
         scratch_shapes=list(scratch.values()),
         compiler_params=pltpu.CompilerParams(
-            collective_id=0, has_side_effects=True, vmem_limit_bytes=67043328
+            collective_id=0, has_side_effects=True, vmem_limit_bytes=58 * 1024 * 1024
         ),
     )(iterate, source_term, conductivity)
+    return settled(new, res)
+
+
+def settle(new_in, res_in, new_out, res_out, sems):
+    copies = [
+        pltpu.make_async_copy(held, out, sems.at[k])
+        for k, (held, out) in enumerate(((new_in, new_out), (res_in, res_out)))
+    ]
+    for copy in copies:
+        copy.start()
+    for copy in copies:
+        copy.wait()
+
+
+def settled(new, res):
+    hbm = pl.BlockSpec(memory_space=pltpu.HBM)
+    out = jax.ShapeDtypeStruct(new.shape, jnp.float32)
+    return pl.pallas_call(
+        settle,
+        out_shape=(out, out),
+        in_specs=[pl.BlockSpec(memory_space=pltpu.VMEM)] * 2,
+        out_specs=(hbm, hbm),
+        scratch_shapes=[pltpu.SemaphoreType.DMA((2,))],
+        compiler_params=pltpu.CompilerParams(vmem_limit_bytes=1024 * 1024),
+    )(new, res)
 
 
 def solution(mesh):

time: 52.7 us -> 50.9 us (0.966)
  local copies, waits for them, and re-layouts: 2.74 us -> 0 us
  Pallas kernels: 49 us -> 50.2 us
    unnamed x4 -> x0, local copies, waits for them, and re-layouts: 2.74 us -> none
    pallas_call x0 -> x1, Pallas kernels: none -> 0.99 us  [settled(): pl.pallas_call(settle, out_shape=(out, out), in_specs=[pl.BlockSpec(memor...]
where the time goes in v6:
time: 50.9 us; the launch traced here: 50.8 us
  Pallas kernels  50.2 us (99%)
  between operations  0.64 us (1%)
    pallas_call x1, Pallas kernels, shards(): pl.pallas_call(functools.partial(kernel, tm_size, space_size, names), out...  49.2 us

profile of v6, /device:TPU:5, one launch (start us, length us, event | category | flops | bytes accessed | tf_op | source)
XLA Modules:
  0.0 50.8 jit_solution(8254163127249307870)
XLA Ops:
  0.6 49.2 %shard_map.50 = (f32[1,1,16,16,512]{4,3,2,1,0:T(8,128)S(1)}, f32[1,1,16,16,512]{4,3,2,1,0:T(8,128)S(1)}) custom-call(f32[1,1,16,16,512]{4,3,2,1,0:T(8,128)} %refs_0_.1, f32[1,1,16,16,512]{4,3,2,1,0:T(8,128)} %refs_1_.1, f32[1,16,16,512]{3,2,1,0:T(8,128)} %refs_2_.1), custom_call_target="tpu_custom_call" | custom-call | tf_op jit(solution)/shard_map/pallas_call | solution.py:1009
  49.8 1.0 %shard_map.51 = (f32[1,1,16,16,512]{4,3,2,1,0:T(8,128)}, f32[1,1,16,16,512]{4,3,2,1,0:T(8,128)}) custom-call(f32[1,1,16,16,512]{4,3,2,1,0:T(8,128)S(1)} %get-tuple-element.4.new_in, f32[1,1,16,16,512]{4,3,2,1,0:T(8,128)S(1)} %get-tuple-element.5.res_in), custom_call_target="tpu_custom_call" | custom-call | tf_op jit(solution)/shard_map/pallas_call | solution.py:1036
